TPU v7x, 32 devices: a whole 2x2x4 slice. The times are simulated.
32 devices in a mesh: tm: 4 (over z), height: 4 (over y, core), heads: 2 (over x).
Axes of the slice: x: 2, y: 2, z: 4, core: 2. Of those that a mesh axis runs over, the one named last changes fastest.
Arguments:
- grad_output: bfloat16 [4, 4, 384, 3072], P('tm', 'height', None, 'heads'), may hold values from -6 to 6
- out_weight: bfloat16 [2048, 3072], P(None, 'heads'), may hold values from -0.109375 to 0.109375
- queries: bfloat16 [4, 4, 384, 2048], P('tm', 'height', None, 'heads'), may hold values from -24 to 24
- key_states: bfloat16 [4, 4, 384, 2048], P('tm', 'height', None, 'heads'), may hold values from -4 to 4
- value_states: bfloat16 [4, 4, 384, 2048], P('tm', 'height', None, 'heads'), may hold values from -6 to 6
- window: int32 [4, 4, 1, 27], replicated, may hold values from 0 to 1, as said below
Outputs:
- query_grad: bfloat16 [4, 4, 384, 2048], P('tm', 'height', None, 'heads')
- key_grad: bfloat16 [4, 4, 384, 2048], P('tm', 'height', None, 'heads')
- value_grad: bfloat16 [4, 4, 384, 2048], P('tm', 'height', None, 'heads')
Inputs may be any that keep to these rules, and one draw needn't show every extreme that they name: window[t, h, w, 9(a+1) + 3(b+1) + (c+1)] is 1 where query tile (t, h, w) attends key tile (t+a, h+b, w+c), a, b, c each -1, 0 or 1; it is 1 at index 13 (the tile itself) and 0 where the key tile lies outside the video.
All inputs are finite; a program needn't handle non-finite values.
Results may differ from a plain program's by a relative error of at most 0.02.
Values may be sent and summed in bfloat16 or wider, within the bound.
No kernel may reach another device: no remote copies, remote signals or barrier semaphores. Data moves between devices by JAX's collectives and lax.ppermute only.
A program may use at most 128 MiB of HBM per device.

v0:
```python
import jax
import jax.numpy as jnp
from jax import lax
from jax.sharding import PartitionSpec as P

HD = 128
TILE = 384
TW = 1


lowest = -1e30


def extended(cells, sides, width):
    for axis, dim in sides:
        count = lax.axis_size(axis)
        ends = count - 1
        head = lax.slice_in_dim(cells, 0, width, axis=dim)
        tail = lax.slice_in_dim(cells, cells.shape[dim] - width, cells.shape[dim], axis=dim)
        cells = jnp.concatenate(
            [
                lax.ppermute(tail, axis, [(i, (i + 1) % count) for i in range(ends)]),
                cells,
                lax.ppermute(head, axis, [((i + 1) % count, i) for i in range(ends)]),
            ],
            axis=dim,
        )
    return cells


def tile_slice(matrix):
    return matrix.reshape(TILE, -1, HD)


def arrange(live_flags):
    ordering = jnp.argsort(1 - live_flags.astype(jnp.int32), stable=True)
    return (ordering, jnp.sum(live_flags.astype(jnp.int32)))


def key_flags(window, time_index, height_index, time_count, height_count):
    item_index = jnp.arange(TW * 27, dtype=jnp.int32)
    tile_number = item_index // 27
    offset = item_index % 27
    source_time = time_index - (offset // 9 - 1)
    source_height = height_index - (offset // 3 % 3 - 1)
    source_tile = tile_number - (offset % 3 - 1)
    inside = (
        (source_time >= 0)
        & (source_time < time_count)
        & (source_height >= 0)
        & (source_height < height_count)
        & (source_tile >= 0)
        & (source_tile < TW)
    )
    looked = window[
        jnp.clip(source_time, 0, time_count - 1),
        jnp.clip(source_height, 0, height_count - 1),
        jnp.clip(source_tile, 0, TW - 1),
        offset,
    ]
    return inside & (looked == 1)


def online_update(previous, scores, slopes):
    highest = jnp.maximum(previous[0], jnp.max(scores, axis=2))
    factor = jnp.exp(previous[0] - highest)
    weights = jnp.exp(scores - highest[:, :, None])
    return jnp.stack(
        [
            highest,
            previous[1] * factor + jnp.sum(weights, axis=2),
            previous[2] * factor + jnp.sum(weights * slopes, axis=2),
        ]
    )


def pair_scores(query_tile, grad_tile, key_tile, value_tile, scaling):
    scores = (
        jnp.einsum("qhd,khd->hqk", query_tile, key_tile, preferred_element_type=jnp.float32)
        * scaling
    )
    slopes = jnp.einsum("qhd,khd->hqk", grad_tile, value_tile, preferred_element_type=jnp.float32)
    return (scores, slopes)


def query_passes(query_rows, grad_rows, neighbours, ordering, live_count, scaling):
    tokens, features = query_rows.shape
    heads_here = features // HD

    def fetch(item_index):
        tile_number = item_index // 27
        offset = item_index % 27
        column = tile_number + offset % 3 - 1
        fetched = lax.dynamic_slice(
            neighbours, (offset // 9, offset // 3 % 3, column * TILE, 0), (1, 1, TILE, 2 * features)
        )
        fetched = fetched.reshape(TILE, 2, heads_here, HD)
        scores, slopes = pair_scores(
            tile_slice(query_rows), tile_slice(grad_rows), fetched[:, 0], fetched[:, 1], scaling
        )
        return (tile_number, fetched[:, 0], scores, slopes)

    def gather_stats(counter, current):
        tile_number, key_tile, scores, slopes = fetch(ordering[counter])
        renewed = online_update(current, scores, slopes)
        return renewed

    start_state = jnp.zeros((3, heads_here, tokens), jnp.float32).at[0].set(lowest)
    final_state = lax.fori_loop(0, live_count, gather_stats, start_state)
    log_total = final_state[0] + jnp.log(final_state[1])
    mean_slope = final_state[2] / final_state[1]

    def gather_query(counter, running):
        tile_number, key_tile, scores, slopes = fetch(ordering[counter])
        probabilities = jnp.exp(scores - log_total[:, :, None])
        score_grads = (probabilities * (slopes - mean_slope[:, :, None])).astype(jnp.bfloat16)
        update = jnp.einsum(
            "hqk,khd->qhd", score_grads, key_tile, preferred_element_type=jnp.float32
        ).reshape(TILE, features)
        return running + update

    query_sum = lax.fori_loop(
        0, live_count, gather_query, jnp.zeros((tokens, features), jnp.float32)
    )
    return (log_total, mean_slope, query_sum)


def key_fetch(item_index, key_rows, value_rows, query_rim, scaling):
    features = key_rows.shape[1]
    heads_here = features // HD
    tile_number = item_index // 27
    offset = item_index % 27
    time_slot = 2 - offset // 9
    height_slot = 2 - offset // 3 % 3
    source = tile_number - offset % 3 + 1
    fetched = lax.dynamic_slice(
        query_rim, (time_slot, height_slot, source * TILE, 0), (1, 1, TILE, 2 * features)
    )
    fetched = fetched.reshape(TILE, 2, heads_here, HD)
    key_tile = tile_slice(key_rows)
    value_tile = tile_slice(value_rows)
    scores, slopes = pair_scores(fetched[:, 0], fetched[:, 1], key_tile, value_tile, scaling)
    return (
        tile_number,
        time_slot,
        height_slot,
        source,
        fetched[:, 0],
        fetched[:, 1],
        key_tile,
        scores,
        slopes,
    )


def owner_grads(key_rows, value_rows, query_rim, stats_rim, ordering, live_count, scaling):
    tokens, features = key_rows.shape
    heads_here = features // HD

    def gather_grads(counter, carried):
        key_sum, value_sum, query_sum = carried
        fetched = key_fetch(ordering[counter], key_rows, value_rows, query_rim, scaling)
        (
            tile_number,
            time_slot,
            height_slot,
            source,
            query_tile,
            grad_tile,
            key_tile,
            scores,
            slopes,
        ) = fetched
        statistics = lax.dynamic_slice(
            stats_rim, (time_slot, height_slot, 0, source * TILE), (1, 1, 2 * heads_here, TILE)
        ).reshape(2, heads_here, TILE)
        probabilities = jnp.exp(scores - statistics[0][:, :, None])
        score_grads = (probabilities * (slopes - statistics[1][:, :, None])).astype(jnp.bfloat16)
        value_part = jnp.einsum(
            "hqk,qhd->khd",
            probabilities.astype(jnp.bfloat16),
            grad_tile,
            preferred_element_type=jnp.float32,
        ).reshape(TILE, features)
        key_part = jnp.einsum(
            "hqk,qhd->khd", score_grads, query_tile, preferred_element_type=jnp.float32
        ).reshape(TILE, features)
        key_sum = key_sum + key_part
        value_sum = value_sum + value_part
        return (key_sum, value_sum, query_sum)

    query_start = jnp.zeros((1,), jnp.float32)
    start_sums = (
        jnp.zeros((tokens, features), jnp.float32),
        jnp.zeros((tokens, features), jnp.float32),
        query_start,
    )
    return lax.fori_loop(0, live_count, gather_grads, start_sums)


def body(grad_output, out_weight, queries, key_states, value_states, window):
    tokens = queries.shape[2]
    features = queries.shape[3]
    heads_here = features // HD
    scaling = HD ** (-0.5)
    grad_rows = grad_output.reshape(tokens, grad_output.shape[3])
    grad_columns = lax.psum_scatter(
        lax.dot_general(
            out_weight, grad_rows, (((1,), (1,)), ((), ())), preferred_element_type=jnp.float32
        ).astype(jnp.bfloat16),
        "heads",
        scatter_dimension=0,
        tiled=True,
    )
    grad_tokens = grad_columns.T
    query_rows = queries.reshape(tokens, features)
    key_rows = key_states.reshape(tokens, features)
    value_rows = value_states.reshape(tokens, features)
    time_index = lax.axis_index("tm")
    height_index = lax.axis_index("height")
    time_count = lax.axis_size("tm")
    height_count = lax.axis_size("height")
    key_order, key_count = arrange(
        key_flags(window, time_index, height_index, time_count, height_count)
    )
    paired = jnp.concatenate([query_rows, grad_tokens], axis=1).reshape(1, 1, tokens, 2 * features)
    query_rim = extended(paired, (("tm", 0), ("height", 1)), 1)
    own_flags = (
        lax.dynamic_slice(window, (time_index, height_index, 0, 0), (1, 1, TW, 27)).reshape(-1) == 1
    )
    own_order, own_count = arrange(own_flags)
    stacked = jnp.concatenate([key_states, value_states], axis=3)
    key_rim = extended(stacked, (("tm", 0), ("height", 1)), 1)
    log_total, mean_slope, query_sum = query_passes(
        query_rows, grad_tokens, key_rim, own_order, own_count, scaling
    )
    statistics = jnp.concatenate([log_total, mean_slope], axis=0).reshape(
        1, 1, 2 * heads_here, tokens
    )
    stats_rim = extended(statistics, (("tm", 0), ("height", 1)), 1)
    key_sum, value_sum, unused = owner_grads(
        key_rows, value_rows, query_rim, stats_rim, key_order, key_count, scaling
    )
    shape = (1, 1, tokens, features)
    query_grad = (scaling * query_sum).astype(jnp.bfloat16).reshape(shape)
    key_grad = (scaling * key_sum).astype(jnp.bfloat16).reshape(shape)
    value_grad = value_sum.astype(jnp.bfloat16).reshape(shape)
    return (query_grad, key_grad, value_grad)


def solution(mesh):
    return jax.shard_map(
        body,
        mesh=mesh,
        in_specs=(
            P("tm", "height", None, "heads"),
            P(None, "heads"),
            P("tm", "height", None, "heads"),
            P("tm", "height", None, "heads"),
            P("tm", "height", None, "heads"),
            P(),
        ),
        out_specs=(
            P("tm", "height", None, "heads"),
            P("tm", "height", None, "heads"),
            P("tm", "height", None, "heads"),
        ),
        check_vma=False,
    )
```

profile of v0, /device:TPU:11, one launch (start us, length us, event | category | flops | bytes accessed | tf_op | source)
XLA Modules:
  0.0 432.5 jit_solution(11021151499279780537)
XLA Ops:
  13.0 3.2 collective-permute-start
  16.2 32.0 %collective-permute-done.1 = bf16[1,1,384,2048]{2,3,1,0:T(8,128)(2,1)S(1)} collective-permute-done((bf16[1,1,384,2048]{2,3,1,0:T(8,128)(2,1)S(1)}, bf16[1,1,384,2048]{2,3,1,0:T(8,128)(2,1)S(1)}, u32[]{:S(2)}, u32[]{:S(2)}) %collective-permute-start.1) | collective-permute-done | bytes 1572896 | tf_op jit(solution)/shard_map/ppermute | solution.py:24
  50.0 4.8 %pad_maximum_fusion.3 = bf16[3,1,384,2048]{2,3,1,0:T(8,128)(2,1)} fusion(bf16[1,1,384,2048]{2,3,1,0:T(8,128)(2,1)S(1)} %collective-permute-done.1, bf16[1,1,384,1024]{2,3,1,0:T(8,128)(2,1)S(1)} %copy.32, bf16[1,1,384,1024]{2,3,1,0:T(8,128)(2,1)S(1)} %copy.31, bf16[1,1,384,2048]{2,3,1,0:T(8,128)(2,1)S(1)} %collective-permute-done), kind=kLoop, calls=%fused_computation.56 | loop fusion | flops 18874368 | bytes 9437184 | tf_op jit(solution)/shard_map/concatenate | solution.py:20
  54.8 3.7 collective-permute-start.3
  58.5 3.0 collective-permute-start.2
  61.6 4.5 %convolution_convert_fusion = bf16[2048,384]{1,0:T(8,128)(2,1)} fusion(bf16[2048,1536]{1,0:T(8,128)(2,1)S(1)} %bitcast.211, bf16[1,1,384,1536]{3,2,1,0:T(8,128)(2,1)S(1)} %copy-done), kind=kOutput, calls=%fused_computation.58 | convolution fusion | flops 2416705536 | bytes 9043968 | tf_op jit(solution)/shard_map/dot_general | solution.py:208
  73.1 20.4 %reduce-scatter.2.cloned.1.call-done = bf16[1024,384]{1,0:T(8,128)(2,1)} async-done(((bf16[2048,384]{1,0:T(8,128)(2,1)}), bf16[1024,384]{1,0:T(8,128)(2,1)}) %reduce-scatter.2.cloned.1.call-update) | async-done | bytes 786448 | tf_op jit(solution)/shard_map/reduce_scatter | solution.py:207
  99.8 3.1 collective-permute-start.4
  103.0 9.1 %collective-permute-done.3 = bf16[3,1,384,2048]{2,3,1,0:T(8,128)(2,1)} collective-permute-done((bf16[3,1,384,2048]{2,3,1,0:T(8,128)(2,1)}, bf16[3,1,384,2048]{2,3,1,0:T(8,128)(2,1)}, u32[]{:S(2)}, u32[]{:S(2)}) %collective-permute-start.3) | collective-permute-done | bytes 4718624 | tf_op jit(solution)/shard_map/ppermute | solution.py:24
  113.0 13.0 %pad_maximum_fusion.1 = bf16[3,3,384,2048]{2,3,1,0:T(8,128)(2,1)} fusion(bf16[3,1,384,2048]{2,3,1,0:T(8,128)(2,1)} %collective-permute-done.3, bf16[1,1,384,2048]{2,3,1,0:T(8,128)(2,1)} %copy-done.11, bf16[1,1,384,1024]{2,3,1,0:T(8,128)(2,1)S(1)} %copy.32, bf16[1,1,384,1024]{2,3,1,0:T(8,128)(2,1)S(1)} %copy-done.10, bf16[1,1,384,2048]{2,3,1,0:T(8,128)(2,1)} %copy-done.12, ...), kind=kLoop, calls=%fused_computation.54 | loop fusion | flops 84934656 | bytes 28311552 | tf_op jit(solution)/shard_map/concatenate | solution.py:20
  126.0 41.6 %while.42 = (s32[]{:T(128)}, f32[3,8,384]{2,1,0:T(8,128)S(1)}, s32[]{:T(128)}, s32[27]{0:T(128)S(1)}, bf16[3,3,384,2048]{2,3,1,0:T(8,128)(2,1)}, /*index=5*/bf16...) while((s32[]{:T(128)}, f32[3,8,384]{2,1,0:T(8,128)S(1)}, ...), condition=%wide.region_7.8_spmd, body=%wide.region_3.7_spmd.sunk | while | flops 614630400 | bytes 22327812 | solution.py:109
  169.5 3.4 collective-permute-start.8
  172.9 5.2 %pad_maximum_fusion.4 = bf16[3,1,384,2048]{2,3,1,0:T(8,128)(2,1)} fusion(bf16[1,1,384,2048]{2,3,1,0:T(8,128)(2,1)} %collective-permute-done.5, bf16[1,1,384,2048]{2,3,1,0:T(8,128)(2,1)} %maximum_bitcast_fusion, bf16[1,1,384,2048]{2,3,1,0:T(8,128)(2,1)} %collective-permute-done.4), kind=kLoop, calls=%fused_computation.57 | loop fusion | flops 4718592 | bytes 9437184 | tf_op jit(solution)/shard_map/concatenate | solution.py:20
  180.0 3.6 collective-permute-start.6
  190.5 94.6 %while.43 = (s32[]{:T(128)}, f32[384,1024]{0,1:T(8,128)}, s32[]{:T(128)}, s32[27]{0:T(128)S(1)}, bf16[3,3,384,2048]{2,3,1,0:T(8,128)(2,1)}, /*index=5*/bf16[1,1,...) while((s32[]{:T(128)}, f32[384,1024]{0,1:T(8,128)}, ...), condition=%wide.region_9.10_spmd, body=%wide.region_8.9_spmd.sunk | while | flops 912261120 | bytes 32268876 | solution.py:122
  197.9 5.2 %fusion.90 = f32[8,128,384]{2,1,0:T(8,128)} fusion(f32[8,384,384]{2,1,0:T(8,128)} %fusion.89, bf16[384,8,128]{0,2,1:T(8,128)(2,1)S(1)} %bitcast.205, f32[8,384]{1,0:T(8,128)S(1)} %get-tuple-element.840, f32[8,384]{1,0:T(8,128)S(1)} %get-tuple-element.838, bf16[384,2,8,128]{0,3,2,1:T(8,128)(2,1)S(1)} %bitcast.197), kind=kOutput, calls=%fused_computation.21.clone.1 | convolution fusion | flops 609878016 | bytes 8675328 | tf_op jit(solution)/shard_map/while/body/hqk,khd->qhd/dot_general | solution.py:117
  203.1 3.3 bitcast_add_fusion.11
  213.5 5.2 %fusion.90 = f32[8,128,384]{2,1,0:T(8,128)} fusion(f32[8,384,384]{2,1,0:T(8,128)} %fusion.89, bf16[384,8,128]{0,2,1:T(8,128)(2,1)S(1)} %bitcast.205, f32[8,384]{1,0:T(8,128)S(1)} %get-tuple-element.840, f32[8,384]{1,0:T(8,128)S(1)} %get-tuple-element.838, bf16[384,2,8,128]{0,3,2,1:T(8,128)(2,1)S(1)} %bitcast.197), kind=kOutput, calls=%fused_computation.21.clone.1 | convolution fusion | flops 609878016 | bytes 8675328 | tf_op jit(solution)/shard_map/while/body/hqk,khd->qhd/dot_general | solution.py:117
  218.7 3.3 bitcast_add_fusion.11
  229.2 5.2 %fusion.90 = f32[8,128,384]{2,1,0:T(8,128)} fusion(f32[8,384,384]{2,1,0:T(8,128)} %fusion.89, bf16[384,8,128]{0,2,1:T(8,128)(2,1)S(1)} %bitcast.205, f32[8,384]{1,0:T(8,128)S(1)} %get-tuple-element.840, f32[8,384]{1,0:T(8,128)S(1)} %get-tuple-element.838, bf16[384,2,8,128]{0,3,2,1:T(8,128)(2,1)S(1)} %bitcast.197), kind=kOutput, calls=%fused_computation.21.clone.1 | convolution fusion | flops 609878016 | bytes 8675328 | tf_op jit(solution)/shard_map/while/body/hqk,khd->qhd/dot_general | solution.py:117
  234.3 3.3 bitcast_add_fusion.11
  244.8 5.2 %fusion.90 = f32[8,128,384]{2,1,0:T(8,128)} fusion(f32[8,384,384]{2,1,0:T(8,128)} %fusion.89, bf16[384,8,128]{0,2,1:T(8,128)(2,1)S(1)} %bitcast.205, f32[8,384]{1,0:T(8,128)S(1)} %get-tuple-element.840, f32[8,384]{1,0:T(8,128)S(1)} %get-tuple-element.838, bf16[384,2,8,128]{0,3,2,1:T(8,128)(2,1)S(1)} %bitcast.197), kind=kOutput, calls=%fused_computation.21.clone.1 | convolution fusion | flops 609878016 | bytes 8675328 | tf_op jit(solution)/shard_map/while/body/hqk,khd->qhd/dot_general | solution.py:117
  250.0 3.3 bitcast_add_fusion.11
  260.4 5.2 %fusion.90 = f32[8,128,384]{2,1,0:T(8,128)} fusion(f32[8,384,384]{2,1,0:T(8,128)} %fusion.89, bf16[384,8,128]{0,2,1:T(8,128)(2,1)S(1)} %bitcast.205, f32[8,384]{1,0:T(8,128)S(1)} %get-tuple-element.840, f32[8,384]{1,0:T(8,128)S(1)} %get-tuple-element.838, bf16[384,2,8,128]{0,3,2,1:T(8,128)(2,1)S(1)} %bitcast.197), kind=kOutput, calls=%fused_computation.21.clone.1 | convolution fusion | flops 609878016 | bytes 8675328 | tf_op jit(solution)/shard_map/while/body/hqk,khd->qhd/dot_general | solution.py:117
  265.6 3.3 bitcast_add_fusion.11
  276.1 5.2 %fusion.90 = f32[8,128,384]{2,1,0:T(8,128)} fusion(f32[8,384,384]{2,1,0:T(8,128)} %fusion.89, bf16[384,8,128]{0,2,1:T(8,128)(2,1)S(1)} %bitcast.205, f32[8,384]{1,0:T(8,128)S(1)} %get-tuple-element.840, f32[8,384]{1,0:T(8,128)S(1)} %get-tuple-element.838, bf16[384,2,8,128]{0,3,2,1:T(8,128)(2,1)S(1)} %bitcast.197), kind=kOutput, calls=%fused_computation.21.clone.1 | convolution fusion | flops 609878016 | bytes 8675328 | tf_op jit(solution)/shard_map/while/body/hqk,khd->qhd/dot_general | solution.py:117
  281.3 3.3 bitcast_add_fusion.11
  285.1 3.1 copy.35
  289.2 13.4 %pad_maximum_fusion.2 = bf16[3,3,384,2048]{2,3,1,0:T(8,128)(2,1)} fusion(bf16[3,1,384,2048]{2,3,1,0:T(8,128)(2,1)} %collective-permute-done.7, bf16[1,1,384,2048]{2,3,1,0:T(8,128)(2,1)} %collective-permute-done.5, bf16[1,1,384,2048]{2,3,1,0:T(8,128)(2,1)} %maximum_bitcast_fusion, bf16[1,1,384,2048]{2,3,1,0:T(8,128)(2,1)} %collective-permute-done.4, ...), kind=kLoop, calls=%fused_computation.55 | loop fusion | flops 28311552 | bytes 28311552 | tf_op jit(solution)/shard_map/concatenate | solution.py:20
  305.2 111.7 %while.44 = (s32[]{:T(128)}, f32[384,1024]{0,1:T(8,128)}, f32[384,1024]{0,1:T(8,128)}, s32[]{:T(128)}, s32[27]{0:T(128)S(1)}, /*index=5*/bf16[3,3,384,2048]{2,3,...) while((s32[]{:T(128)}, f32[384,1024]{0,1:T(8,128)}, ...), condition=%wide.region_13.14_spmd, body=%wide.region_12.13_spmd.sunk | while | flops 1218183168 | bytes 40981120 | solution.py:198
  309.0 3.0 fusion.94
  312.0 4.6 %fusion.95 = f32[8,128,384]{2,1,0:T(8,128)} fusion(f32[8,384,384]{2,1,0:T(8,128)} %fusion.94, f32[8,384]{1,0:T(8,128)S(1)} %get-tuple-element.754, bf16[384,2,8,128]{0,3,2,1:T(8,128)(2,1)S(1)} %bitcast.193), kind=kOutput, calls=%fused_computation.35.clone.1 | convolution fusion | flops 305528832 | bytes 7090176 | tf_op jit(solution)/shard_map/while/body/hqk,qhd->khd/dot_general | solution.py:179
  316.9 5.5 %fusion.96 = f32[8,128,384]{2,1,0:T(8,128)} fusion(f32[8,384,384]{2,1,0:T(8,128)} %fusion.94, bf16[384,8,128]{0,2,1:T(8,128)(2,1)S(1)} %bitcast.204, f32[8,384]{1,0:T(8,128)S(1)} %get-tuple-element.755, f32[8,384]{1,0:T(8,128)S(1)} %get-tuple-element.754, bf16[384,2,8,128]{0,3,2,1:T(8,128)(2,1)S(1)} %bitcast.194), kind=kOutput, calls=%fused_computation.36.clone.1 | convolution fusion | flops 609878016 | bytes 8675328 | tf_op jit(solution)/shard_map/while/body/hqk,qhd->khd/dot_general | solution.py:185
  322.4 5.0 %bitcast_add_fusion.12 = (f32[384,1024]{0,1:T(8,128)}, f32[384,1024]{0,1:T(8,128)}) fusion(f32[384,1024]{0,1:T(8,128)} %get-tuple-element.869, f32[8,128,384]{2,1,0:T(8,128)} %fusion.95, f32[384,1024]{0,1:T(8,128)} %get-tuple-element.868, f32[8,128,384]{2,1,0:T(8,128)} %fusion.96), kind=kLoop, calls=%fused_computation.43.clone.1 | loop fusion | flops 786432 | bytes 9437184 | tf_op jit(solution)/shard_map/while/body/add | solution.py:189
  334.2 4.6 %fusion.95 = f32[8,128,384]{2,1,0:T(8,128)} fusion(f32[8,384,384]{2,1,0:T(8,128)} %fusion.94, f32[8,384]{1,0:T(8,128)S(1)} %get-tuple-element.754, bf16[384,2,8,128]{0,3,2,1:T(8,128)(2,1)S(1)} %bitcast.193), kind=kOutput, calls=%fused_computation.35.clone.1 | convolution fusion | flops 305528832 | bytes 7090176 | tf_op jit(solution)/shard_map/while/body/hqk,qhd->khd/dot_general | solution.py:179
  339.1 5.5 %fusion.96 = f32[8,128,384]{2,1,0:T(8,128)} fusion(f32[8,384,384]{2,1,0:T(8,128)} %fusion.94, bf16[384,8,128]{0,2,1:T(8,128)(2,1)S(1)} %bitcast.204, f32[8,384]{1,0:T(8,128)S(1)} %get-tuple-element.755, f32[8,384]{1,0:T(8,128)S(1)} %get-tuple-element.754, bf16[384,2,8,128]{0,3,2,1:T(8,128)(2,1)S(1)} %bitcast.194), kind=kOutput, calls=%fused_computation.36.clone.1 | convolution fusion | flops 609878016 | bytes 8675328 | tf_op jit(solution)/shard_map/while/body/hqk,qhd->khd/dot_general | solution.py:185
  344.6 5.0 %bitcast_add_fusion.12 = (f32[384,1024]{0,1:T(8,128)}, f32[384,1024]{0,1:T(8,128)}) fusion(f32[384,1024]{0,1:T(8,128)} %get-tuple-element.869, f32[8,128,384]{2,1,0:T(8,128)} %fusion.95, f32[384,1024]{0,1:T(8,128)} %get-tuple-element.868, f32[8,128,384]{2,1,0:T(8,128)} %fusion.96), kind=kLoop, calls=%fused_computation.43.clone.1 | loop fusion | flops 786432 | bytes 9437184 | tf_op jit(solution)/shard_map/while/body/add | solution.py:189
  353.4 3.0 fusion.94
  356.3 4.6 %fusion.95 = f32[8,128,384]{2,1,0:T(8,128)} fusion(f32[8,384,384]{2,1,0:T(8,128)} %fusion.94, f32[8,384]{1,0:T(8,128)S(1)} %get-tuple-element.754, bf16[384,2,8,128]{0,3,2,1:T(8,128)(2,1)S(1)} %bitcast.193), kind=kOutput, calls=%fused_computation.35.clone.1 | convolution fusion | flops 305528832 | bytes 7090176 | tf_op jit(solution)/shard_map/while/body/hqk,qhd->khd/dot_general | solution.py:179
  361.3 5.5 %fusion.96 = f32[8,128,384]{2,1,0:T(8,128)} fusion(f32[8,384,384]{2,1,0:T(8,128)} %fusion.94, bf16[384,8,128]{0,2,1:T(8,128)(2,1)S(1)} %bitcast.204, f32[8,384]{1,0:T(8,128)S(1)} %get-tuple-element.755, f32[8,384]{1,0:T(8,128)S(1)} %get-tuple-element.754, bf16[384,2,8,128]{0,3,2,1:T(8,128)(2,1)S(1)} %bitcast.194), kind=kOutput, calls=%fused_computation.36.clone.1 | convolution fusion | flops 609878016 | bytes 8675328 | tf_op jit(solution)/shard_map/while/body/hqk,qhd->khd/dot_general | solution.py:185
  366.8 5.0 %bitcast_add_fusion.12 = (f32[384,1024]{0,1:T(8,128)}, f32[384,1024]{0,1:T(8,128)}) fusion(f32[384,1024]{0,1:T(8,128)} %get-tuple-element.869, f32[8,128,384]{2,1,0:T(8,128)} %fusion.95, f32[384,1024]{0,1:T(8,128)} %get-tuple-element.868, f32[8,128,384]{2,1,0:T(8,128)} %fusion.96), kind=kLoop, calls=%fused_computation.43.clone.1 | loop fusion | flops 786432 | bytes 9437184 | tf_op jit(solution)/shard_map/while/body/add | solution.py:189
  378.5 4.6 %fusion.95 = f32[8,128,384]{2,1,0:T(8,128)} fusion(f32[8,384,384]{2,1,0:T(8,128)} %fusion.94, f32[8,384]{1,0:T(8,128)S(1)} %get-tuple-element.754, bf16[384,2,8,128]{0,3,2,1:T(8,128)(2,1)S(1)} %bitcast.193), kind=kOutput, calls=%fused_computation.35.clone.1 | convolution fusion | flops 305528832 | bytes 7090176 | tf_op jit(solution)/shard_map/while/body/hqk,qhd->khd/dot_general | solution.py:179
  383.5 5.5 %fusion.96 = f32[8,128,384]{2,1,0:T(8,128)} fusion(f32[8,384,384]{2,1,0:T(8,128)} %fusion.94, bf16[384,8,128]{0,2,1:T(8,128)(2,1)S(1)} %bitcast.204, f32[8,384]{1,0:T(8,128)S(1)} %get-tuple-element.755, f32[8,384]{1,0:T(8,128)S(1)} %get-tuple-element.754, bf16[384,2,8,128]{0,3,2,1:T(8,128)(2,1)S(1)} %bitcast.194), kind=kOutput, calls=%fused_computation.36.clone.1 | convolution fusion | flops 609878016 | bytes 8675328 | tf_op jit(solution)/shard_map/while/body/hqk,qhd->khd/dot_general | solution.py:185
  389.0 5.0 %bitcast_add_fusion.12 = (f32[384,1024]{0,1:T(8,128)}, f32[384,1024]{0,1:T(8,128)}) fusion(f32[384,1024]{0,1:T(8,128)} %get-tuple-element.869, f32[8,128,384]{2,1,0:T(8,128)} %fusion.95, f32[384,1024]{0,1:T(8,128)} %get-tuple-element.868, f32[8,128,384]{2,1,0:T(8,128)} %fusion.96), kind=kLoop, calls=%fused_computation.43.clone.1 | loop fusion | flops 786432 | bytes 9437184 | tf_op jit(solution)/shard_map/while/body/add | solution.py:189
  400.7 4.6 %fusion.95 = f32[8,128,384]{2,1,0:T(8,128)} fusion(f32[8,384,384]{2,1,0:T(8,128)} %fusion.94, f32[8,384]{1,0:T(8,128)S(1)} %get-tuple-element.754, bf16[384,2,8,128]{0,3,2,1:T(8,128)(2,1)S(1)} %bitcast.193), kind=kOutput, calls=%fused_computation.35.clone.1 | convolution fusion | flops 305528832 | bytes 7090176 | tf_op jit(solution)/shard_map/while/body/hqk,qhd->khd/dot_general | solution.py:179
  405.7 5.5 %fusion.96 = f32[8,128,384]{2,1,0:T(8,128)} fusion(f32[8,384,384]{2,1,0:T(8,128)} %fusion.94, bf16[384,8,128]{0,2,1:T(8,128)(2,1)S(1)} %bitcast.204, f32[8,384]{1,0:T(8,128)S(1)} %get-tuple-element.755, f32[8,384]{1,0:T(8,128)S(1)} %get-tuple-element.754, bf16[384,2,8,128]{0,3,2,1:T(8,128)(2,1)S(1)} %bitcast.194), kind=kOutput, calls=%fused_computation.36.clone.1 | convolution fusion | flops 609878016 | bytes 8675328 | tf_op jit(solution)/shard_map/while/body/hqk,qhd->khd/dot_general | solution.py:185
  411.2 5.0 %bitcast_add_fusion.12 = (f32[384,1024]{0,1:T(8,128)}, f32[384,1024]{0,1:T(8,128)}) fusion(f32[384,1024]{0,1:T(8,128)} %get-tuple-element.869, f32[8,128,384]{2,1,0:T(8,128)} %fusion.95, f32[384,1024]{0,1:T(8,128)} %get-tuple-element.868, f32[8,128,384]{2,1,0:T(8,128)} %fusion.96), kind=kLoop, calls=%fused_computation.43.clone.1 | loop fusion | flops 786432 | bytes 9437184 | tf_op jit(solution)/shard_map/while/body/add | solution.py:189
  416.9 3.2 copy.37
  (223 shorter events, 131.4 us)
Async XLA Ops:
  7.2 54.4 %copy-start = (bf16[1,1,384,1536]{3,2,1,0:T(8,128)(2,1)S(1)}, bf16[1,1,384,1536]{3,2,1,0:T(8,128)(2,1)}, u32[]{:S(2)}) copy-start(bf16[1,1,384,1536]{3,2,1,0:T(8,128)(2,1)} %param.14) | copy-start | bytes 3538948
  7.2 86.3 %reduce-scatter.2.cloned.1.call-start = ((), (), s32[]{:S(2)}) async-start(), calls=%async_computation.1 | async-start | bytes 2359296 | tf_op jit(solution)/shard_map/reduce_scatter | solution.py:207
  10.3 39.7 %copy-start.9 = (bf16[1,1,384,1024]{2,3,1,0:T(8,128)(2,1)}, bf16[1,1,384,1024]{2,3,1,0:T(8,128)(2,1)S(1)}, u32[]{:S(2)}) copy-start(bf16[1,1,384,1024]{2,3,1,0:T(8,128)(2,1)S(1)} %copy.31) | copy-start | bytes 2359300
  10.3 51.3 %slice-start = ((s8[6291456]{0:T(1024)(128)(4,1)}), s8[4194304]{0:T(1024)(128)(4,1)S(1)}, s32[]{:S(2)}) async-start(s8[6291456]{0:T(1024)(128)(4,1)} %bitcast.210), calls=%async_computation.2 | async-start | bytes 8388608
  10.5 51.1 %slice-start.1 = ((s8[6291456]{0:T(1024)(128)(4,1)}), s8[2097152]{0:T(1024)(128)(4,1)S(1)}, s32[]{:S(2)}) async-start(s8[6291456]{0:T(1024)(128)(4,1)} %bitcast.210), calls=%async_computation.3 | async-start | bytes 4194304
  10.5 37.7 %collective-permute-start.1 = (bf16[1,1,384,2048]{2,3,1,0:T(8,128)(2,1)S(1)}, bf16[1,1,384,2048]{2,3,1,0:T(8,128)(2,1)S(1)}, u32[]{:S(2)}, u32[]{:S(2)}) collective-permute-start(bf16[1,1,384,2048]{2,3,1,0:T(8,128)(2,1)S(1)} %pad_maximum_fusion.5), channel_id=1, source_target_pairs={{8,0},{16,8},{24,16},{9,1},{17,9},{25,17},{10,2},{18,10},{26,18},{... | collective-permute-start | bytes 4718600 | tf_op jit(solution)/shard_map/ppermute | solution.py:24
  13.0 37.0 %collective-permute-start = (bf16[1,1,384,2048]{2,3,1,0:T(8,128)(2,1)S(1)}, bf16[1,1,384,2048]{2,3,1,0:T(8,128)(2,1)S(1)}, u32[]{:S(2)}, u32[]{:S(2)}) collective-permute-start(bf16[1,1,384,2048]{2,3,1,0:T(8,128)(2,1)S(1)} %pad_maximum_fusion.5), channel_id=1, source_target_pairs={{0,8},{8,16},{16,24},{1,9},{9,17},{17,25},{2,10},{10,18},{18,26},{... | collective-permute-start | bytes 4718600 | tf_op jit(solution)/shard_map/ppermute | solution.py:22
  48.2 6.6 %copy-start.11 = (bf16[1,1,384,2048]{2,3,1,0:T(8,128)(2,1)}, bf16[1,1,384,2048]{2,3,1,0:T(8,128)(2,1)S(1)}, u32[]{:S(2)}) copy-start(bf16[1,1,384,2048]{2,3,1,0:T(8,128)(2,1)S(1)} %collective-permute-done.1) | copy-start | bytes 4718596
  50.0 8.5 %copy-start.12 = (bf16[1,1,384,2048]{2,3,1,0:T(8,128)(2,1)}, bf16[1,1,384,2048]{2,3,1,0:T(8,128)(2,1)S(1)}, u32[]{:S(2)}) copy-start(bf16[1,1,384,2048]{2,3,1,0:T(8,128)(2,1)S(1)} %collective-permute-done) | copy-start | bytes 4718596
  54.8 11.4 %copy-start.3 = (s32[4,4,1,27]{3,2,1,0:T(1,128)S(1)}, s32[4,4,1,27]{3,2,1,0:T(1,128)}, u32[]{:S(2)}) copy-start(s32[4,4,1,27]{3,2,1,0:T(1,128)} %param.19) | copy-start | bytes 5188
  54.8 13.1 %copy-start.2 = (bf16[1,1,384,1024]{3,2,1,0:T(8,128)(2,1)S(1)}, bf16[1,1,384,1024]{3,2,1,0:T(8,128)(2,1)}, u32[]{:S(2)}) copy-start(bf16[1,1,384,1024]{3,2,1,0:T(8,128)(2,1)} %param.16) | copy-start | bytes 2359300
  54.8 57.2 %collective-permute-start.3 = (bf16[3,1,384,2048]{2,3,1,0:T(8,128)(2,1)}, bf16[3,1,384,2048]{2,3,1,0:T(8,128)(2,1)}, u32[]{:S(2)}, u32[]{:S(2)}) collective-permute-start(bf16[3,1,384,2048]{2,3,1,0:T(8,128)(2,1)} %pad_maximum_fusion.3), channel_id=1, source_target_pairs={{2,0},{4,2},{6,4},{3,1},{5,3},{7,5},{10,8},{12,10},{14,12},{11,9},... | collective-permute-start | bytes 14155784 | tf_op jit(solution)/shard_map/ppermute | solution.py:24
  58.5 54.4 %collective-permute-start.2 = (bf16[3,1,384,2048]{2,3,1,0:T(8,128)(2,1)}, bf16[3,1,384,2048]{2,3,1,0:T(8,128)(2,1)}, u32[]{:S(2)}, u32[]{:S(2)}) collective-permute-start(bf16[3,1,384,2048]{2,3,1,0:T(8,128)(2,1)} %pad_maximum_fusion.3), channel_id=1, source_target_pairs={{0,2},{2,4},{4,6},{1,3},{3,5},{5,7},{8,10},{10,12},{12,14},{9,11},... | collective-permute-start | bytes 14155784 | tf_op jit(solution)/shard_map/ppermute | solution.py:22
  66.2 46.8 %copy-start.10 = (bf16[1,1,384,1024]{2,3,1,0:T(8,128)(2,1)S(1)}, bf16[1,1,384,1024]{2,3,1,0:T(8,128)(2,1)}, u32[]{:S(2)}) copy-start(bf16[1,1,384,1024]{2,3,1,0:T(8,128)(2,1)} %copy-done.9) | copy-start | bytes 2359300
  97.5 28.4 %copy-start.14 = (f32[3,8,384]{2,1,0:T(8,128)S(1)}, f32[3,8,384]{2,1,0:T(8,128)}, u32[]{:S(2)}) copy-start(f32[3,8,384]{2,1,0:T(8,128)} %constant.330.clone.1) | copy-start | bytes 110596
  97.5 75.3 %collective-permute-start.5 = (bf16[1,1,384,2048]{2,3,1,0:T(8,128)(2,1)}, bf16[1,1,384,2048]{2,3,1,0:T(8,128)(2,1)}, u32[]{:S(2)}, u32[]{:S(2)}) collective-permute-start(bf16[1,1,384,2048]{2,3,1,0:T(8,128)(2,1)} %maximum_bitcast_fusion), channel_id=1, source_target_pairs={{8,0},{16,8},{24,16},{9,1},{17,9},{25,17},{10,2},{18,10},{26,18},{... | collective-permute-start | bytes 4718600 | tf_op jit(solution)/shard_map/ppermute | solution.py:24
  99.8 73.1 %collective-permute-start.4 = (bf16[1,1,384,2048]{2,3,1,0:T(8,128)(2,1)}, bf16[1,1,384,2048]{2,3,1,0:T(8,128)(2,1)}, u32[]{:S(2)}, u32[]{:S(2)}) collective-permute-start(bf16[1,1,384,2048]{2,3,1,0:T(8,128)(2,1)} %maximum_bitcast_fusion), channel_id=1, source_target_pairs={{0,8},{8,16},{16,24},{1,9},{9,17},{17,25},{2,10},{10,18},{18,26},{... | collective-permute-start | bytes 4718600 | tf_op jit(solution)/shard_map/ppermute | solution.py:22
  167.6 16.1 %collective-permute-start.9 = (f32[1,1,16,384]{3,2,1,0:T(8,128)S(1)}, f32[1,1,16,384]{3,2,1,0:T(8,128)S(1)}, u32[]{:S(2)}, u32[]{:S(2)}) collective-permute-start(f32[1,1,16,384]{3,2,1,0:T(8,128)S(1)} %maximum_bitcast_fusion.1), channel_id=1, source_target_pairs={{8,0},{16,8},{24,16},{9,1},{17,9},{25,17},{10,2},{18,10},{26,18},{... | collective-permute-start | bytes 73736 | tf_op jit(solution)/shard_map/ppermute | solution.py:24
  169.5 14.2 %collective-permute-start.8 = (f32[1,1,16,384]{3,2,1,0:T(8,128)S(1)}, f32[1,1,16,384]{3,2,1,0:T(8,128)S(1)}, u32[]{:S(2)}, u32[]{:S(2)}) collective-permute-start(f32[1,1,16,384]{3,2,1,0:T(8,128)S(1)} %maximum_bitcast_fusion.1), channel_id=1, source_target_pairs={{0,8},{8,16},{16,24},{1,9},{9,17},{17,25},{2,10},{10,18},{18,26},{... | collective-permute-start | bytes 73736 | tf_op jit(solution)/shard_map/ppermute | solution.py:22
  178.1 111.1 %collective-permute-start.7 = (bf16[3,1,384,2048]{2,3,1,0:T(8,128)(2,1)}, bf16[3,1,384,2048]{2,3,1,0:T(8,128)(2,1)}, u32[]{:S(2)}, u32[]{:S(2)}) collective-permute-start(bf16[3,1,384,2048]{2,3,1,0:T(8,128)(2,1)} %pad_maximum_fusion.4), channel_id=1, source_target_pairs={{2,0},{4,2},{6,4},{3,1},{5,3},{7,5},{10,8},{12,10},{14,12},{11,9},... | collective-permute-start | bytes 14155784 | tf_op jit(solution)/shard_map/ppermute | solution.py:24
  180.0 109.2 %collective-permute-start.6 = (bf16[3,1,384,2048]{2,3,1,0:T(8,128)(2,1)}, bf16[3,1,384,2048]{2,3,1,0:T(8,128)(2,1)}, u32[]{:S(2)}, u32[]{:S(2)}) collective-permute-start(bf16[3,1,384,2048]{2,3,1,0:T(8,128)(2,1)} %pad_maximum_fusion.4), channel_id=1, source_target_pairs={{0,2},{2,4},{4,6},{1,3},{3,5},{5,7},{8,10},{10,12},{12,14},{9,11},... | collective-permute-start | bytes 14155784 | tf_op jit(solution)/shard_map/ppermute | solution.py:22
  183.7 104.5 %collective-permute-start.11 = (f32[3,1,16,384]{3,2,1,0:T(8,128)S(1)}, f32[3,1,16,384]{3,2,1,0:T(8,128)S(1)}, u32[]{:S(2)}, u32[]{:S(2)}) collective-permute-start(f32[3,1,16,384]{3,2,1,0:T(8,128)S(1)} %pad_maximum_fusion.7), channel_id=1, source_target_pairs={{2,0},{4,2},{6,4},{3,1},{5,3},{7,5},{10,8},{12,10},{14,12},{11,9},... | collective-permute-start | bytes 221192 | tf_op jit(solution)/shard_map/ppermute | solution.py:24
  186.6 101.7 %collective-permute-start.10 = (f32[3,1,16,384]{3,2,1,0:T(8,128)S(1)}, f32[3,1,16,384]{3,2,1,0:T(8,128)}, u32[]{:S(2)}, u32[]{:S(2)}) collective-permute-start(f32[3,1,16,384]{3,2,1,0:T(8,128)S(1)} %pad_maximum_fusion.7), channel_id=1, source_target_pairs={{0,2},{2,4},{4,6},{1,3},{3,5},{5,7},{8,10},{10,12},{12,14},{9,11},... | collective-permute-start | bytes 221192 | tf_op jit(solution)/shard_map/ppermute | solution.py:22
  191.3 1.7 copy-start.7
  203.1 3.3 copy-start.8
  207.0 1.7 copy-start.7
  218.7 3.3 copy-start.8
  222.6 1.7 copy-start.7
  234.3 3.3 copy-start.8
  238.2 1.7 copy-start.7
  250.0 3.3 copy-start.8
  253.9 1.7 copy-start.7
  265.6 3.3 copy-start.8
  269.5 1.7 copy-start.7
  281.3 3.3 copy-start.8
  289.1 16.1 %copy-start.4 = (bf16[1,1,384,1024]{3,2,1,0:T(8,128)(2,1)S(1)}, bf16[1,1,384,1024]{3,2,1,0:T(8,128)(2,1)}, u32[]{:S(2)}) copy-start(bf16[1,1,384,1024]{3,2,1,0:T(8,128)(2,1)} %param.18) | copy-start | bytes 2359300
  289.1 16.1 %copy-start.5 = (bf16[1,1,384,1024]{3,2,1,0:T(8,128)(2,1)S(1)}, bf16[1,1,384,1024]{3,2,1,0:T(8,128)(2,1)}, u32[]{:S(2)}) copy-start(bf16[1,1,384,1024]{3,2,1,0:T(8,128)(2,1)} %param.17) | copy-start | bytes 2359300
  322.4 5.0 %copy-start.6 = (bf16[1,1,384,1024]{3,2,1,0:T(8,128)(2,1)S(1)}, bf16[1,1,384,1024]{3,2,1,0:T(8,128)(2,1)}, u32[]{:S(2)}) copy-start(bf16[1,1,384,1024]{3,2,1,0:T(8,128)(2,1)} %get-tuple-element.927) | copy-start | bytes 2359300 | tf_op jit(solution)/shard_map/while
  344.6 5.0 %copy-start.6 = (bf16[1,1,384,1024]{3,2,1,0:T(8,128)(2,1)S(1)}, bf16[1,1,384,1024]{3,2,1,0:T(8,128)(2,1)}, u32[]{:S(2)}) copy-start(bf16[1,1,384,1024]{3,2,1,0:T(8,128)(2,1)} %get-tuple-element.927) | copy-start | bytes 2359300 | tf_op jit(solution)/shard_map/while
  366.8 5.0 %copy-start.6 = (bf16[1,1,384,1024]{3,2,1,0:T(8,128)(2,1)S(1)}, bf16[1,1,384,1024]{3,2,1,0:T(8,128)(2,1)}, u32[]{:S(2)}) copy-start(bf16[1,1,384,1024]{3,2,1,0:T(8,128)(2,1)} %get-tuple-element.927) | copy-start | bytes 2359300 | tf_op jit(solution)/shard_map/while
  389.0 5.0 %copy-start.6 = (bf16[1,1,384,1024]{3,2,1,0:T(8,128)(2,1)S(1)}, bf16[1,1,384,1024]{3,2,1,0:T(8,128)(2,1)}, u32[]{:S(2)}) copy-start(bf16[1,1,384,1024]{3,2,1,0:T(8,128)(2,1)} %get-tuple-element.927) | copy-start | bytes 2359300 | tf_op jit(solution)/shard_map/while
  411.2 5.0 %copy-start.6 = (bf16[1,1,384,1024]{3,2,1,0:T(8,128)(2,1)S(1)}, bf16[1,1,384,1024]{3,2,1,0:T(8,128)(2,1)}, u32[]{:S(2)}) copy-start(bf16[1,1,384,1024]{3,2,1,0:T(8,128)(2,1)} %get-tuple-element.927) | copy-start | bytes 2359300 | tf_op jit(solution)/shard_map/while
  416.9 5.8 %copy-start.13 = (f32[384,1024]{1,0:T(8,128)S(1)}, f32[384,1024]{1,0:T(8,128)}, u32[]{:S(2)}) copy-start(f32[384,1024]{1,0:T(8,128)} %copy.35) | copy-start | bytes 4718596
  416.9 8.8 %copy-start.1 = (bf16[1,1,384,1536]{3,2,1,0:T(8,128)(2,1)S(1)}, bf16[1,1,384,1536]{3,2,1,0:T(8,128)(2,1)}, u32[]{:S(2)}) copy-start(bf16[1,1,384,1536]{3,2,1,0:T(8,128)(2,1)} %param.14) | copy-start | bytes 3538948
Sparse Core Ops, SparseCore 0:
  66.3 27.0 reduce-scatter.1
where the time goes:
time: 435 us; the launch traced here: 432 us
  matrix products  132 us (30%)
  other arithmetic  97.3 us (22%)
  waiting for transfers between devices  64.2 us (15%)
  local copies, waits for them, and re-layouts  64 us (15%)
  starting transfers between devices  34.3 us (8%)
  loops' own time  25.8 us (6%)
  between operations  14.4 us (3%)
    ppermute x6, waiting for transfers between devices, extended(): lax.ppermute(head, axis, [((i + 1) % count, i) for i in range(ends)])  41.1 us
    concatenate x6, other arithmetic, extended(): jnp.concatenate([lax.ppermute(tail, axis, [(i, (i + 1) % count) for i in...  37.3 us
    dot_general x6, matrix products, gather_query(): jnp.einsum('hqk,khd->qhd', score_grads, key_tile, preferred_element_type=...  31.1 us
    dot_general x5, matrix products, gather_grads(): jnp.einsum('hqk,qhd->khd', score_grads, query_tile, preferred_element_typ...  27.6 us
    dot_general x12, matrix products, pair_scores(): jnp.einsum('qhd,khd->hqk', grad_tile, value_tile, preferred_element_type=...  26.1 us
    add x5, other arithmetic, gather_grads(): value_sum = value_sum + value_part  24.8 us
    dot_general x5, matrix products, gather_grads(): jnp.einsum('hqk,qhd->khd', probabilities.astype(jnp.bfloat16), grad_tile,...  22.9 us
    reduce_scatter x1, waiting for transfers between devices, body(): lax.psum_scatter(lax.dot_general(out_weight, grad_rows, (((1,), (1,)), ((...  20.4 us
  transfers between devices with their start and end apart: 13, of which 5 were waited for; matrix products, arithmetic and copies ran while one was open for 36% of the time, Pallas kernels for 0%

commit v1 on v0

--- a/solution.py
+++ b/solution.py
@@ -1,9 +1,378 @@
+import functools
+
 import jax
 import jax.numpy as jnp
 from jax import lax
+from jax.experimental import pallas as pl
+from jax.experimental.pallas import tpu as pltpu
 from jax.sharding import PartitionSpec as P
 
+
 HD = 128
+LOG2E = 1.4426950408889634
+NT = (((1,), (1,)), ((), ()))
+TN = (((0,), (0,)), ((), ()))
+CHUNK = 192
+BF16 = jnp.bfloat16
+F32 = jnp.float32
+
+
+def params(limit=56 << 20):
+    return pltpu.CompilerParams(vmem_limit_bytes=limit)
+
+
+def vmem():
+    return pl.BlockSpec(memory_space=pltpu.VMEM)
+
+
+def smem():
+    return pl.BlockSpec(memory_space=pltpu.SMEM)
+
+
+def hbm():
+    return pl.BlockSpec(memory_space=pltpu.HBM)
+
+
+def cost(moved, flops=0, transcendentals=0):
+    return pl.CostEstimate(
+        flops=int(flops), transcendentals=int(transcendentals), bytes_accessed=int(moved)
+    )
+
+
+def shaped(shape, kind=BF16):
+    return jax.ShapeDtypeStruct(shape, kind)
+
+
+def run_copies(copies):
+    for copy in copies:
+        copy.start()
+    for copy in copies:
+        copy.wait()
+
+
+def split_kernel(pieces, group, position, key, value, query, *outs):
+    me = position[1]
+    for slot in range(pieces):
+        first = pl.multiple_of((me ^ slot) * group * HD, group * HD)
+        for n in range(group):
+            columns = pl.ds(first + n * HD, HD)
+            outs[n * pieces + slot][0] = key[:, columns]
+            outs[n * pieces + slot][1] = value[:, columns]
+        outs[group * pieces + slot][0] = query[:, pl.ds(first, group * HD)]
+
+
+def split(key, value, query, position, pieces, group):
+    rows = key.shape[0]
+    flat = pl.pallas_call(
+        functools.partial(split_kernel, pieces, group),
+        out_shape=[shaped((2, rows, HD))] * (group * pieces)
+        + [shaped((1, rows, group * HD))] * pieces,
+        in_specs=[smem()] + [vmem()] * 3,
+        out_specs=[vmem()] * ((group + 1) * pieces),
+        name="split_heads",
+        cost_estimate=cost(12 * key.size),
+    )(position, key, value, query)
+    return [flat[i * pieces : (i + 1) * pieces] for i in range(group + 1)]
+
+
+def join_kernel(pieces, group, position, *refs):
+    query_out, key_out, value_out = refs[-3:]
+    me = position[1]
+    for slot in range(pieces):
+        first = pl.multiple_of((me ^ slot) * group * HD, group * HD)
+        for n in range(group):
+            columns = pl.ds(first + n * HD, HD)
+            query_out[:, columns] = refs[slot][n]
+            key_out[:, columns] = refs[(n + 1) * pieces + slot][0]
+            value_out[:, columns] = refs[(n + 1) * pieces + slot][1]
+
+
+def join(query_pieces, kv_pieces, position):
+    pieces = len(query_pieces)
+    group, rows = len(kv_pieces), query_pieces[0].shape[1]
+    flat = list(query_pieces) + [piece for part in kv_pieces for piece in part]
+    return pl.pallas_call(
+        functools.partial(join_kernel, pieces, group),
+        out_shape=[shaped((rows, group * pieces * HD))] * 3,
+        in_specs=[smem()] + [vmem()] * len(flat),
+        out_specs=[vmem()] * 3,
+        name="join_heads",
+        cost_estimate=cost(12 * rows * group * pieces * HD),
+    )(position, *flat)
+
+
+def swap(pieces):
+    count = len(pieces)
+    swapped = [pieces[0]]
+    for slot in range(1, count):
+        swapped.append(lax.ppermute(pieces[slot], "height", [(i, i ^ slot) for i in range(count)]))
+    return swapped
+
+
+def exchange(first, second):
+    count = lax.axis_size("tm")
+    arrived = []
+    for parity, block in ((0, first), (1, second)):
+        pairs = [(i, i + 1) for i in range(parity, count - 1, 2)]
+        arrived.append(
+            lax.ppermute(block, "tm", pairs + [(target, source) for source, target in pairs])
+        )
+    return arrived
+
+
+def add_kernel(pieces, group, head, position, full, arrived, *refs):
+    mine, sem = refs[-2:]
+    me, side = position[1], position[2]
+    copies = []
+    for slot in range(pieces):
+        start = ((side * pieces + (me ^ slot)) * group + head) * HD
+        rows = pl.ds(pl.multiple_of(start, HD), HD)
+        copies.append(pltpu.make_async_copy(full.at[rows], mine.at[slot], sem.at[slot]))
+    run_copies(copies)
+    for slot in range(pieces):
+        refs[slot][...] = (mine[slot].astype(F32) + arrived[me ^ slot].astype(F32)).astype(BF16)
+
+
+def add_parts(full, arrived, head, group, position):
+    pieces, rows, tokens = arrived.shape
+    return pl.pallas_call(
+        functools.partial(add_kernel, pieces, group, head),
+        out_shape=[shaped((rows, tokens))] * pieces,
+        in_specs=[smem(), hbm(), vmem()],
+        out_specs=[vmem()] * pieces,
+        scratch_shapes=[
+            pltpu.VMEM((pieces, rows, tokens), BF16),
+            pltpu.SemaphoreType.DMA((pieces,)),
+        ],
+        name="add_parts",
+        cost_estimate=cost(6 * arrived.size),
+    )(position, full, arrived)
+
+
+def total_kernel(own_ref, low_ref, high_ref, *outs):
+    for slot, out in enumerate(outs):
+        out[...] = (
+            own_ref[slot].astype(F32) + (low_ref[slot].astype(F32) + high_ref[slot].astype(F32))
+        ).astype(BF16)
+
+
+def total(own, low, high):
+    pieces, planes, rows, width = own.shape
+    return pl.pallas_call(
+        total_kernel,
+        out_shape=[shaped((planes, rows, width))] * pieces,
+        in_specs=[vmem()] * 3,
+        out_specs=[vmem()] * pieces,
+        name="total_grads",
+        cost_estimate=cost(8 * own.size),
+    )(own, low, high)
+
+
+def attend_kernel(rows_count, head, position, window, *refs):
+    q_in, g_in = refs[:rows_count], refs[rows_count : 2 * rows_count]
+    kv_in = refs[2 * rows_count : 2 * rows_count + 3]
+    earlier = rows_count if head else 0
+    dq_in = refs[2 * rows_count + 3 : 2 * rows_count + 3 + earlier]
+    rest = refs[2 * rows_count + 3 + earlier :]
+    dq_out, kv_out = rest[:rows_count], rest[rows_count : rows_count + 3]
+    q_all, g_all, kv_all, acc, kv_low, dq_all, s_buf, d_buf, order, sem = rest[rows_count + 3 :]
+    slot = pl.program_id(0)
+    tile = q_all.shape[1]
+    scaling = HD**-0.5
+    factor = scaling * LOG2E
+    chunks = [slice(c * CHUNK, (c + 1) * CHUNK) for c in range(tile // CHUNK)]
+    time_index, me = position[0], position[1]
+
+    def loads():
+        copies = []
+        for i in range(rows_count):
+            columns = pl.ds(head * HD, HD)
+            copies.append(
+                pltpu.make_async_copy(q_in[i].at[0, :, columns], q_all.at[i], sem.at[i])
+            )
+            copies.append(
+                pltpu.make_async_copy(g_in[i], g_all.at[i], sem.at[rows_count + i])
+            )
+            if head:
+                copies.append(
+                    pltpu.make_async_copy(
+                        dq_in[i], dq_all.at[i, pl.ds(0, head)], sem.at[2 * rows_count + 3 + i]
+                    )
+                )
+        for i in range(3):
+            part = pl.ds(i * rows_count, rows_count)
+            copies.append(
+                pltpu.make_async_copy(kv_in[i], kv_all.at[part], sem.at[2 * rows_count + i])
+            )
+        return copies
+
+    def stores():
+        copies = []
+        for i in range(3):
+            part = pl.ds(i * rows_count, rows_count)
+            copies.append(
+                pltpu.make_async_copy(kv_low.at[part], kv_out[i], sem.at[2 * rows_count + i])
+            )
+        for i in range(rows_count):
+            copies.append(pltpu.make_async_copy(dq_all.at[i], dq_out[i], sem.at[i]))
+        return copies
+
+    @pl.when(slot == 0)
+    def _():
+        copies = loads()
+        for copy in copies:
+            copy.start()
+        acc[...] = jnp.zeros_like(acc)
+        for copy in copies:
+            copy.wait()
+
+    row = me ^ slot
+    odd = time_index % 2
+    block = (2 - 2 * odd, 1, 2 * odd)
+    count = jnp.int32(0)
+    for a in range(3):
+        for b in range(3):
+            order[count] = block[a] * rows_count + ((row + b - 1) ^ me)
+            count = count + window[time_index, row, 0, 9 * a + 3 * b + 1]
+
+    query = q_all[slot]
+    grad = g_all[slot]
+
+    def scores(i, highest):
+        where = order[i]
+        for part in chunks:
+            s = lax.dot_general(kv_all[where, 0, part, :], query, NT, preferred_element_type=F32)
+            s_buf[i, part, :] = s
+            highest = jnp.maximum(highest, jnp.max(s.reshape(-1, 8, tile), axis=0))
+        return highest
+
+    highest = lax.fori_loop(0, count, scores, jnp.full((8, tile), -1e30, F32))
+    highest = jnp.max(highest, axis=0, keepdims=True)
+
+    def sums(i, carried):
+        mass, weighted = carried
+        where = order[i]
+        for part in chunks:
+            slopes = jnp.dot(kv_all[where, 1, part, :], grad, preferred_element_type=F32)
+            weights = jnp.exp2((s_buf[i, part, :] - highest) * factor)
+            s_buf[i, part, :] = weights
+            d_buf[i, part, :] = slopes
+            mass = mass + jnp.sum(weights.reshape(-1, 8, tile), axis=0)
+            weighted = weighted + jnp.sum((weights * slopes).reshape(-1, 8, tile), axis=0)
+        return mass, weighted
+
+    zero = jnp.zeros((8, tile), F32)
+    mass, weighted = lax.fori_loop(0, count, sums, (zero, zero))
+    mass = jnp.sum(mass, axis=0, keepdims=True)
+    weighted = jnp.sum(weighted, axis=0, keepdims=True)
+    inverse = 1.0 / mass
+    delta = weighted * inverse
+
+    def grads(i, query_sum):
+        where = order[i]
+        for part in chunks:
+            weights = s_buf[i, part, :] * inverse
+            slopes = (weights * (d_buf[i, part, :] - delta)).astype(BF16)
+            weights = weights.astype(BF16)
+            acc[where, 1, part, :] += lax.dot_general(
+                weights, grad, NT, preferred_element_type=F32
+            )
+            acc[where, 0, part, :] += jnp.dot(slopes, query, preferred_element_type=F32)
+            query_sum = query_sum + lax.dot_general(
+                kv_all[where, 0, part, :], slopes, TN, preferred_element_type=F32
+            )
+        return query_sum
+
+    query_sum = lax.fori_loop(0, count, grads, jnp.zeros((HD, tile), F32))
+    dq_all[slot, head] = (scaling * query_sum).T.astype(BF16)
+
+    @pl.when(slot == rows_count - 1)
+    def _():
+        kv_low[:, 0] = (scaling * acc[:, 0]).astype(BF16)
+        kv_low[:, 1] = acc[:, 1].astype(BF16)
+        run_copies(stores())
+
+
+def attend(q_pieces, g_pieces, kv_three, dq_pieces, position, window, head):
+    rows_count = len(q_pieces)
+    tile = q_pieces[0].shape[1]
+    stack = (rows_count, 2, tile, HD)
+    flops = rows_count * 3 * 10 * tile * tile * HD
+    result = pl.pallas_call(
+        functools.partial(attend_kernel, rows_count, head),
+        out_shape=[shaped((head + 1, tile, HD))] * rows_count + [shaped(stack)] * 3,
+        grid_spec=pltpu.PrefetchScalarGridSpec(
+            num_scalar_prefetch=2,
+            grid=(rows_count,),
+            in_specs=[hbm()] * (2 * rows_count + 3 + len(dq_pieces)),
+            out_specs=[hbm()] * (rows_count + 3),
+            scratch_shapes=[
+                pltpu.VMEM((rows_count, tile, HD), BF16),
+                pltpu.VMEM((rows_count, HD, tile), BF16),
+                pltpu.VMEM((3 * rows_count, 2, tile, HD), BF16),
+                pltpu.VMEM((3 * rows_count, 2, tile, HD), F32),
+                pltpu.VMEM((3 * rows_count, 2, tile, HD), BF16),
+                pltpu.VMEM((rows_count, head + 1, tile, HD), BF16),
+                pltpu.VMEM((9, tile, tile), F32),
+                pltpu.VMEM((9, tile, tile), F32),
+                pltpu.SMEM((16,), jnp.int32),
+                pltpu.SemaphoreType.DMA((3 * rows_count + 3,)),
+            ],
+        ),
+        compiler_params=params(),
+        name="attend",
+        cost_estimate=cost(28 * tile * HD * rows_count, flops, flops // (10 * HD)),
+    )(position, window, *q_pieces, *g_pieces, *kv_three, *dq_pieces)
+    return result[:rows_count], result[rows_count:]
+
+
+def fast_body(grad_output, out_weight, queries, key_states, value_states, window):
+    tokens, features = queries.shape[2], queries.shape[3]
+    pieces = lax.axis_size("height")
+    group = features // (pieces * HD)
+    sides = lax.axis_size("heads")
+    position = jnp.stack([lax.axis_index(name) for name in ("tm", "height", "heads")])
+    position = position.astype(jnp.int32)
+    heads = range(group)
+
+    cut = split(
+        key_states.reshape(tokens, features),
+        value_states.reshape(tokens, features),
+        queries.reshape(tokens, features),
+        position,
+        pieces,
+        group,
+    )
+    kv_pieces = [swap(cut[n]) for n in heads]
+    full = lax.dot_general(
+        out_weight, grad_output.reshape(tokens, -1), NT, preferred_element_type=F32
+    ).astype(BF16)
+    other = lax.dynamic_index_in_dim(
+        full.reshape(sides, pieces, group, HD, tokens), 1 - position[2], 0, keepdims=False
+    )
+    arrived = []
+    for n in heads:
+        arrived.append(lax.ppermute(other[:, n], "heads", [(0, 1), (1, 0)]))
+    query_pieces = swap(cut[group])
+    grad_pieces = []
+    for n in heads:
+        parts = add_parts(full, arrived[n], n, group, position)
+        grad_pieces.append(swap(parts))
+    three = []
+    for n in heads:
+        stack = jnp.stack(kv_pieces[n])
+        near, far = exchange(stack, stack)
+        three.append([near, stack, far])
+    dq, back = [], []
+    for n in heads:
+        dq, partials = attend(query_pieces, grad_pieces[n], three[n], dq, position, window, n)
+        near, far = exchange(partials[0], partials[2])
+        sums = total(partials[1], near, far)
+        back.append(swap(sums))
+    outs = join(swap(dq), back, position)
+    return tuple(out.reshape(1, 1, tokens, features) for out in outs)
+
+
 TILE = 384
 TW = 1
 
@@ -101,7 +470,7 @@
         return (tile_number, fetched[:, 0], scores, slopes)
 
     def gather_stats(counter, current):
-        tile_number, key_tile, scores, slopes = fetch(ordering[counter])
+        _, _, scores, slopes = fetch(ordering[counter])
         renewed = online_update(current, scores, slopes)
         return renewed
 
@@ -111,7 +480,7 @@
     mean_slope = final_state[2] / final_state[1]
 
     def gather_query(counter, running):
-        tile_number, key_tile, scores, slopes = fetch(ordering[counter])
+        _, key_tile, scores, slopes = fetch(ordering[counter])
         probabilities = jnp.exp(scores - log_total[:, :, None])
         score_grads = (probabilities * (slopes - mean_slope[:, :, None])).astype(jnp.bfloat16)
         update = jnp.einsum(
@@ -160,17 +529,7 @@
     def gather_grads(counter, carried):
         key_sum, value_sum, query_sum = carried
         fetched = key_fetch(ordering[counter], key_rows, value_rows, query_rim, scaling)
-        (
-            tile_number,
-            time_slot,
-            height_slot,
-            source,
-            query_tile,
-            grad_tile,
-            key_tile,
-            scores,
-            slopes,
-        ) = fetched
+        (_, time_slot, height_slot, source, query_tile, grad_tile, _, scores, slopes) = fetched
         statistics = lax.dynamic_slice(
             stats_rim, (time_slot, height_slot, 0, source * TILE), (1, 1, 2 * heads_here, TILE)
         ).reshape(2, heads_here, TILE)
@@ -238,7 +597,7 @@
         1, 1, 2 * heads_here, tokens
     )
     stats_rim = extended(statistics, (("tm", 0), ("height", 1)), 1)
-    key_sum, value_sum, unused = owner_grads(
+    key_sum, value_sum, _ = owner_grads(
         key_rows, value_rows, query_rim, stats_rim, key_order, key_count, scaling
     )
     shape = (1, 1, tokens, features)
@@ -248,9 +607,23 @@
     return (query_grad, key_grad, value_grad)
 
 
+def fits(mesh):
+    height, heads = mesh.shape["height"], mesh.shape["heads"]
+
+    def chosen(grad_output, out_weight, queries, key_states, value_states, window):
+        features = queries.shape[3]
+        power = height & (height - 1) == 0
+        fast = heads == 2 and power and features % (height * HD) == 0 and window.shape[2] == 1
+        fast = fast and features == 2 * height * HD
+        plan = fast_body if fast else body
+        return plan(grad_output, out_weight, queries, key_states, value_states, window)
+
+    return chosen
+
+
 def solution(mesh):
     return jax.shard_map(
-        body,
+        fits(mesh),
         mesh=mesh,
         in_specs=(
             P("tm", "height", None, "heads"),

time: 435 us -> 138 us (0.32)
  the two profiles are of different devices: /device:TPU:11 before, /device:TPU:0 now
where the time goes in v1:
time: 138 us; the launch traced here: 137 us
  Pallas kernels  43.4 us (31%)
  waiting for transfers between devices  43.4 us (31%)
  starting transfers between devices  37.5 us (27%)
  matrix products  6.24 us (5%)
  local copies, waits for them, and re-layouts  3.49 us (3%)
  other arithmetic  1.89 us (1%)
    ppermute x24, waiting for transfers between devices, swap(): lax.ppermute(pieces[slot], 'height', [(i, i ^ slot) for i in range(count)])  31.7 us
    pallas_call x2, Pallas kernels, attend(): pl.pallas_call(functools.partial(attend_kernel, rows_count, head), out_sh...  25.1 us
    ppermute x8, starting transfers between devices, exchange(): lax.ppermute(block, 'tm', pairs + [(target, source) for source, target in...  18.6 us
    ppermute x24, starting transfers between devices, swap(): lax.ppermute(pieces[slot], 'height', [(i, i ^ slot) for i in range(count)])  15.7 us
    ppermute x8, waiting for transfers between devices, exchange(): lax.ppermute(block, 'tm', pairs + [(target, source) for source, target in...  11.7 us
    dot_general x1, matrix products, fast_body(): lax.dot_general(out_weight, grad_output.reshape(tokens, -1), NT, preferre...  6.24 us
    pallas_call x2, Pallas kernels, add_parts(): pl.pallas_call(functools.partial(add_kernel, pieces, group, head), out_sh...  5.78 us
    pallas_call x2, Pallas kernels, total(): pl.pallas_call(total_kernel, out_shape=[shaped((planes, rows, width))] *...  5.16 us
  transfers between devices with their start and end apart: 34, of which 11 were waited for; matrix products, arithmetic and copies ran while one was open for 6% of the time, Pallas kernels for 26%

profile of v1, /device:TPU:0, one launch (start us, length us, event | category | flops | bytes accessed | tf_op | source)
XLA Modules:
  0.0 136.9 jit_solution(2794742615846025695)
XLA Ops:
  0.7 0.7 pad_add_fusion.position
  1.3 3.5 %split_heads.1 = (bf16[2,384,128]{2,1,0:T(8,128)(2,1)}, bf16[2,384,128]{2,1,0:T(8,128)(2,1)}, bf16[2,384,128]{2,1,0:T(8,128)(2,1)}, bf16[2,384,128]{2,1,0:T(8,12...) custom-call(s32[3]{0:T(128)} %pad_add_fusion.position, ...), custom_call_target="tpu_custom_call" | custom-call | bytes 4718592 | tf_op jit(solution)/shard_map/split_heads/pallas_call | solution.py:66
  4.8 0.5 collective-permute-start
  5.3 2.6 %collective-permute-start.1 = (bf16[1,384,256]{2,1,0:T(8,128)(2,1)}, bf16[1,384,256]{2,1,0:T(8,128)(2,1)}, u32[]{:S(2)}, u32[]{:S(2)}) collective-permute-start(bf16[1,384,256]{2,1,0:T(8,128)(2,1)} %get-tuple-element.50), channel_id=1, source_target_pairs={{0,4},{2,6},{4,0},{6,2},{1,5},{3,7},{5,1},{7,3},{8,12},{10,14},{12... | collective-permute-start | bytes 589832 | tf_op jit(solution)/shard_map/ppermute | solution.py:108
  8.4 6.2 %convolution_convert_fusion.full = bf16[2048,384]{1,0:T(8,128)(2,1)S(1)} fusion(bf16[2048,1536]{1,0:T(8,128)(2,1)} %param.7, bf16[1,1,384,1536]{3,2,1,0:T(8,128)(2,1)S(1)} %copy-done), kind=kOutput, calls=%fused_computation | convolution fusion | flops 2416705536 | bytes 9043968 | tf_op jit(solution)/shard_map/dot_general | solution.py:347
  14.8 1.0 copy-done.23
  15.8 1.7 %collective-permute-start.17 = (bf16[2,384,128]{2,1,0:T(8,128)(2,1)S(1)}, bf16[2,384,128]{2,1,0:T(8,128)(2,1)S(1)}, u32[]{:S(2)}, u32[]{:S(2)}) collective-permute-start(bf16[2,384,128]{2,1,0:T(8,128)(2,1)S(1)} %copy-done.23), channel_id=1, source_target_pairs={{0,4},{2,6},{4,0},{6,2},{1,5},{3,7},{5,1},{7,3},{8,12},{10,14},{12... | collective-permute-start | bytes 589832 | tf_op jit(solution)/shard_map/ppermute | solution.py:108
  17.6 0.7 copy-done.14
  18.4 5.2 %collective-permute-done.17 = bf16[2,384,128]{2,1,0:T(8,128)(2,1)S(1)} collective-permute-done((bf16[2,384,128]{2,1,0:T(8,128)(2,1)S(1)}, bf16[2,384,128]{2,1,0:T(8,128)(2,1)S(1)}, u32[]{:S(2)}, u32[]{:S(2)}) %collective-permute-start.17) | collective-permute-done | bytes 196640 | tf_op jit(solution)/shard_map/ppermute | solution.py:108
  23.6 1.7 %collective-permute-start.12 = (bf16[4,128,384]{2,1,0:T(8,128)(2,1)S(1)}, bf16[4,128,384]{2,1,0:T(8,128)(2,1)S(1)}, u32[]{:S(2)}, u32[]{:S(2)}) collective-permute-start(bf16[4,128,384]{2,1,0:T(8,128)(2,1)S(1)} %get-tuple-element.93), channel_id=1, source_target_pairs={{0,1},{1,0},{2,3},{3,2},{4,5},{5,4},{6,7},{7,6},{8,9},{9,8},{10,11... | collective-permute-start | bytes 1179656 | tf_op jit(solution)/shard_map/ppermute | solution.py:355
  25.3 1.5 %collective-permute-done.18 = bf16[2,384,128]{2,1,0:T(8,128)(2,1)S(1)} collective-permute-done((bf16[2,384,128]{2,1,0:T(8,128)(2,1)}, bf16[2,384,128]{2,1,0:T(8,128)(2,1)S(1)}, u32[]{:S(2)}, u32[]{:S(2)}) %collective-permute-start.18) | collective-permute-done | bytes 196640 | tf_op jit(solution)/shard_map/ppermute | solution.py:108
  26.8 2.0 %collective-permute-start.9 = (bf16[2,384,128]{2,1,0:T(8,128)(2,1)S(1)}, bf16[2,384,128]{2,1,0:T(8,128)(2,1)S(1)}, u32[]{:S(2)}, u32[]{:S(2)}) collective-permute-start(bf16[2,384,128]{2,1,0:T(8,128)(2,1)S(1)} %copy-done.21), channel_id=1, source_target_pairs={{0,6},{2,4},{4,2},{6,0},{1,7},{3,5},{5,3},{7,1},{8,14},{10,12},{12... | collective-permute-start | bytes 589832 | tf_op jit(solution)/shard_map/ppermute | solution.py:108
  28.9 1.6 %collective-permute-start.20 = (bf16[4,2,384,128]{3,2,1,0:T(8,128)(2,1)S(1)}, bf16[4,2,384,128]{3,2,1,0:T(8,128)(2,1)}, u32[]{:S(2)}, u32[]{:S(2)}) collective-permute-start(bf16[4,2,384,128]{3,2,1,0:T(8,128)(2,1)S(1)} %pad_maximum_fusion.1.refs_9_), channel_id=1, source_target_pairs={{8,16},{16,8},{9,17},{17,9},{10,18},{18,10},{11,19},{19,11},{12,20... | collective-permute-start | bytes 2359304 | tf_op jit(solution)/shard_map/ppermute | solution.py:118
  30.4 3.6 %collective-permute-start.19 = (bf16[4,2,384,128]{3,2,1,0:T(8,128)(2,1)S(1)}, bf16[4,2,384,128]{3,2,1,0:T(8,128)(2,1)}, u32[]{:S(2)}, u32[]{:S(2)}) collective-permute-start(bf16[4,2,384,128]{3,2,1,0:T(8,128)(2,1)S(1)} %pad_maximum_fusion.1.refs_9_), channel_id=1, source_target_pairs={{0,8},{16,24},{8,0},{24,16},{1,9},{17,25},{9,1},{25,17},{2,10},{18... | collective-permute-start | bytes 2359304 | tf_op jit(solution)/shard_map/ppermute | solution.py:118
  34.0 1.6 %collective-permute-start.3 = (bf16[4,128,384]{2,1,0:T(8,128)(2,1)S(1)}, bf16[4,128,384]{2,1,0:T(8,128)(2,1)}, u32[]{:S(2)}, u32[]{:S(2)}) collective-permute-start(bf16[4,128,384]{2,1,0:T(8,128)(2,1)S(1)} %get-tuple-element.94), channel_id=1, source_target_pairs={{0,1},{1,0},{2,3},{3,2},{4,5},{5,4},{6,7},{7,6},{8,9},{9,8},{10,11... | collective-permute-start | bytes 1179656 | tf_op jit(solution)/shard_map/ppermute | solution.py:355
  35.6 1.1 pad_maximum_fusion.refs_9_
  36.7 4.0 %collective-permute-done.2.refs_3_ = bf16[1,384,256]{2,1,0:T(8,128)(2,1)S(1)} collective-permute-done((bf16[1,384,256]{2,1,0:T(8,128)(2,1)S(1)}, bf16[1,384,256]{2,1,0:T(8,128)(2,1)S(1)}, u32[]{:S(2)}, u32[]{:S(2)}) %collective-permute-start.2) | collective-permute-done | bytes 196640 | tf_op jit(solution)/shard_map/ppermute | solution.py:108
  40.7 1.5 %collective-permute-start.11 = (bf16[4,2,384,128]{3,2,1,0:T(8,128)(2,1)S(1)}, bf16[4,2,384,128]{3,2,1,0:T(8,128)(2,1)}, u32[]{:S(2)}, u32[]{:S(2)}) collective-permute-start(bf16[4,2,384,128]{3,2,1,0:T(8,128)(2,1)S(1)} %pad_maximum_fusion.refs_9_), channel_id=1, source_target_pairs={{8,16},{16,8},{9,17},{17,9},{10,18},{18,10},{11,19},{19,11},{12,20... | collective-permute-start | bytes 2359304 | tf_op jit(solution)/shard_map/ppermute | solution.py:118
  42.3 1.9 %collective-permute-start.10 = (bf16[4,2,384,128]{3,2,1,0:T(8,128)(2,1)S(1)}, bf16[4,2,384,128]{3,2,1,0:T(8,128)(2,1)}, u32[]{:S(2)}, u32[]{:S(2)}) collective-permute-start(bf16[4,2,384,128]{3,2,1,0:T(8,128)(2,1)S(1)} %pad_maximum_fusion.refs_9_), channel_id=1, source_target_pairs={{0,8},{16,24},{8,0},{24,16},{1,9},{17,25},{9,1},{25,17},{2,10},{18... | collective-permute-start | bytes 2359304 | tf_op jit(solution)/shard_map/ppermute | solution.py:118
  44.2 2.9 %add_parts.3 = (bf16[128,384]{1,0:T(8,128)(2,1)}, bf16[128,384]{1,0:T(8,128)(2,1)}, bf16[128,384]{1,0:T(8,128)(2,1)}, bf16[128,384]{1,0:T(8,128)(2,1)}) custom-call(s32[3]{0:T(128)} %pad_add_fusion.position, bf16[2048,384]{1,0:T(8,128)(2,1)} %copy-done.1, bf16[4,128,384]{2,1,0:T(8,128)(2,1)} %copy-done.7), custom_call_target="tpu_custom_call" | custom-call | bytes 1179648 | tf_op jit(solution)/shard_map/add_parts/pallas_call | solution.py:138
  47.1 1.5 %collective-permute-done.13.refs_5_ = bf16[128,384]{1,0:T(8,128)(2,1)S(1)} collective-permute-done((bf16[128,384]{1,0:T(8,128)(2,1)}, bf16[128,384]{1,0:T(8,128)(2,1)S(1)}, u32[]{:S(2)}, u32[]{:S(2)}) %collective-permute-start.13) | collective-permute-done | bytes 98336 | tf_op jit(solution)/shard_map/ppermute | solution.py:108
  48.6 0.7 collective-permute-start.14
  49.4 4.3 %collective-permute-done.14.refs_6_ = bf16[128,384]{1,0:T(8,128)(2,1)S(1)} collective-permute-done((bf16[128,384]{1,0:T(8,128)(2,1)}, bf16[128,384]{1,0:T(8,128)(2,1)S(1)}, u32[]{:S(2)}, u32[]{:S(2)}) %collective-permute-start.14) | collective-permute-done | bytes 98336 | tf_op jit(solution)/shard_map/ppermute | solution.py:108
  53.7 2.9 %add_parts.2 = (bf16[128,384]{1,0:T(8,128)(2,1)}, bf16[128,384]{1,0:T(8,128)(2,1)}, bf16[128,384]{1,0:T(8,128)(2,1)}, bf16[128,384]{1,0:T(8,128)(2,1)}) custom-call(s32[3]{0:T(128)} %pad_add_fusion.position, bf16[2048,384]{1,0:T(8,128)(2,1)} %copy-done.1, bf16[4,128,384]{2,1,0:T(8,128)(2,1)} %collective-permute-done.3.arrived), custom_call_target="tpu_custom_call" | custom-call | bytes 1179648 | tf_op jit(solution)/shard_map/add_parts/pallas_call | solution.py:138
  56.6 1.9 %collective-permute-done.15.refs_7_ = bf16[128,384]{1,0:T(8,128)(2,1)S(1)} collective-permute-done((bf16[128,384]{1,0:T(8,128)(2,1)}, bf16[128,384]{1,0:T(8,128)(2,1)S(1)}, u32[]{:S(2)}, u32[]{:S(2)}) %collective-permute-start.15) | collective-permute-done | bytes 98336 | tf_op jit(solution)/shard_map/ppermute | solution.py:108
  58.6 1.1 collective-permute-start.5
  59.7 0.8 collective-permute-start.6
  60.5 12.4 %attend.2 = (bf16[1,384,128]{2,1,0:T(8,128)(2,1)}, bf16[1,384,128]{2,1,0:T(8,128)(2,1)}, bf16[1,384,128]{2,1,0:T(8,128)(2,1)}, bf16[1,384,128]{2,1,0:T(8,128)(2,...) custom-call(s32[3]{0:T(128)} %pad_add_fusion.position, ...), custom_call_target="tpu_custom_call" | custom-call | flops 2264924160 | bytes 5505024 | tf_op jit(solution)/shard_map/attend/pallas_call | solution.py:301
  72.9 2.5 %collective-permute-start.24 = (bf16[4,2,384,128]{3,2,1,0:T(8,128)(2,1)}, bf16[4,2,384,128]{3,2,1,0:T(8,128)(2,1)S(1)}, u32[]{:S(2)}, u32[]{:S(2)}) collective-permute-start(bf16[4,2,384,128]{3,2,1,0:T(8,128)(2,1)} %get-tuple-element.77), channel_id=1, source_target_pairs={{0,8},{16,24},{8,0},{24,16},{1,9},{17,25},{9,1},{25,17},{2,10},{18... | collective-permute-start | bytes 2359304 | tf_op jit(solution)/shard_map/ppermute | solution.py:118
  75.4 0.7 collective-permute-start.25
  76.2 0.6 copy-done.26
  76.8 12.7 %attend.3 = (bf16[2,384,128]{2,1,0:T(8,128)(2,1)}, bf16[2,384,128]{2,1,0:T(8,128)(2,1)}, bf16[2,384,128]{2,1,0:T(8,128)(2,1)}, bf16[2,384,128]{2,1,0:T(8,128)(2,...) custom-call(s32[3]{0:T(128)} %pad_add_fusion.position, ...), custom_call_target="tpu_custom_call" | custom-call | flops 2264924160 | bytes 5505024 | tf_op jit(solution)/shard_map/attend/pallas_call | solution.py:301
  89.5 5.2 %collective-permute-start.29 = (bf16[4,2,384,128]{3,2,1,0:T(8,128)(2,1)}, bf16[4,2,384,128]{3,2,1,0:T(8,128)(2,1)S(1)}, u32[]{:S(2)}, u32[]{:S(2)}) collective-permute-start(bf16[4,2,384,128]{3,2,1,0:T(8,128)(2,1)} %get-tuple-element.84), channel_id=1, source_target_pairs={{0,8},{16,24},{8,0},{24,16},{1,9},{17,25},{9,1},{25,17},{2,10},{18... | collective-permute-start | bytes 2359304 | tf_op jit(solution)/shard_map/ppermute | solution.py:118
  94.7 1.6 %collective-permute-start.30 = (bf16[4,2,384,128]{3,2,1,0:T(8,128)(2,1)}, bf16[4,2,384,128]{3,2,1,0:T(8,128)(2,1)}, u32[]{:S(2)}, u32[]{:S(2)}) collective-permute-start(bf16[4,2,384,128]{3,2,1,0:T(8,128)(2,1)} %get-tuple-element.85), channel_id=1, source_target_pairs={{8,16},{16,8},{9,17},{17,9},{10,18},{18,10},{11,19},{19,11},{12,20... | collective-permute-start | bytes 2359304 | tf_op jit(solution)/shard_map/ppermute | solution.py:118
  96.3 1.3 collective-permute-start.22
  97.6 0.6 collective-permute-start.23
  98.5 2.6 %total_grads.2 = (bf16[2,384,128]{2,1,0:T(8,128)(2,1)}, bf16[2,384,128]{2,1,0:T(8,128)(2,1)}, bf16[2,384,128]{2,1,0:T(8,128)(2,1)}, bf16[2,384,128]{2,1,0:T(8,128)(2,1)}) custom-call(bf16[4,2,384,128]{3,2,1,0:T(8,128)(2,1)} %get-tuple-element.76.own_ref, bf16[4,2,384,128]{3,2,1,0:T(8,128)(2,1)} %copy-done.4, bf16[4,2,384,128]{3,2,1,0:T(8,128)(2,1)} %copy-done.5), custom_call_target="tpu_custom_call" | custom-call | bytes 3145728 | tf_op jit(solution)/shard_map/total_grads/pallas_call | solution.py:161
  101.1 11.7 %collective-permute-done.29.low_ref = bf16[4,2,384,128]{3,2,1,0:T(8,128)(2,1)S(1)} collective-permute-done((bf16[4,2,384,128]{3,2,1,0:T(8,128)(2,1)}, bf16[4,2,384,128]{3,2,1,0:T(8,128)(2,1)S(1)}, u32[]{:S(2)}, u32[]{:S(2)}) %collective-permute-start.29) | collective-permute-done | bytes 786464 | tf_op jit(solution)/shard_map/ppermute | solution.py:118
  112.8 1.3 collective-permute-start.27
  114.0 2.6 %total_grads.3 = (bf16[2,384,128]{2,1,0:T(8,128)(2,1)}, bf16[2,384,128]{2,1,0:T(8,128)(2,1)}, bf16[2,384,128]{2,1,0:T(8,128)(2,1)}, bf16[2,384,128]{2,1,0:T(8,128)(2,1)}) custom-call(bf16[4,2,384,128]{3,2,1,0:T(8,128)(2,1)} %get-tuple-element.83.own_ref, bf16[4,2,384,128]{3,2,1,0:T(8,128)(2,1)} %copy-done.6, ...), custom_call_target="tpu_custom_call" | custom-call | bytes 3145728 | tf_op jit(solution)/shard_map/total_grads/pallas_call | solution.py:161
  116.6 0.7 collective-permute-start.28
  117.6 1.2 collective-permute-start.32
  119.1 1.7 %collective-permute-done.27.refs_6_ = bf16[2,384,128]{2,1,0:T(8,128)(2,1)S(1)} collective-permute-done((bf16[2,384,128]{2,1,0:T(8,128)(2,1)}, bf16[2,384,128]{2,1,0:T(8,128)(2,1)S(1)}, u32[]{:S(2)}, u32[]{:S(2)}) %collective-permute-start.27) | collective-permute-done | bytes 196640 | tf_op jit(solution)/shard_map/ppermute | solution.py:108
  120.8 3.2 %collective-permute-done.28.refs_7_ = bf16[2,384,128]{2,1,0:T(8,128)(2,1)S(1)} collective-permute-done((bf16[2,384,128]{2,1,0:T(8,128)(2,1)S(1)}, bf16[2,384,128]{2,1,0:T(8,128)(2,1)S(1)}, u32[]{:S(2)}, u32[]{:S(2)}) %collective-permute-start.28) | collective-permute-done | bytes 196640 | tf_op jit(solution)/shard_map/ppermute | solution.py:108
  124.0 5.3 %collective-permute-done.32.refs_10_ = bf16[2,384,128]{2,1,0:T(8,128)(2,1)S(1)} collective-permute-done((bf16[2,384,128]{2,1,0:T(8,128)(2,1)}, bf16[2,384,128]{2,1,0:T(8,128)(2,1)S(1)}, u32[]{:S(2)}, u32[]{:S(2)}) %collective-permute-start.32) | collective-permute-done | bytes 196640 | tf_op jit(solution)/shard_map/ppermute | solution.py:108
  129.2 3.2 %collective-permute-done.33.refs_11_ = bf16[2,384,128]{2,1,0:T(8,128)(2,1)S(1)} collective-permute-done((bf16[2,384,128]{2,1,0:T(8,128)(2,1)}, bf16[2,384,128]{2,1,0:T(8,128)(2,1)S(1)}, u32[]{:S(2)}, u32[]{:S(2)}) %collective-permute-start.33) | collective-permute-done | bytes 196640 | tf_op jit(solution)/shard_map/ppermute | solution.py:108
  132.4 0.7 copy-done.17
  133.1 3.8 %join_heads.1 = (bf16[384,1024]{1,0:T(8,128)(2,1)}, bf16[384,1024]{1,0:T(8,128)(2,1)}, bf16[384,1024]{1,0:T(8,128)(2,1)}) custom-call(s32[3]{0:T(128)} %pad_add_fusion.position, bf16[2,384,128]{2,1,0:T(8,128)(2,1)} %get-tuple-element.72.refs_0_, bf16[2,384,128]{2,1,0:T(8,128)(2,1)} %collective-permute-done.21.refs_1_, ...), custom_call_target="tpu_custom_call" | custom-call | bytes 4718592 | tf_op jit(solution)/shard_map/join_heads/pallas_call | solution.py:94
  (94 shorter events, 2.1 us)
Async XLA Ops:
  0.6 7.8 %copy-start = (bf16[1,1,384,1536]{3,2,1,0:T(8,128)(2,1)S(1)}, bf16[1,1,384,1536]{3,2,1,0:T(8,128)(2,1)}, u32[]{:S(2)}) copy-start(bf16[1,1,384,1536]{3,2,1,0:T(8,128)(2,1)} %param.6) | copy-start | bytes 3538948
  4.8 10.0 %collective-permute-start = (bf16[1,384,256]{2,1,0:T(8,128)(2,1)}, bf16[1,384,256]{2,1,0:T(8,128)(2,1)S(1)}, u32[]{:S(2)}, u32[]{:S(2)}) collective-permute-start(bf16[1,384,256]{2,1,0:T(8,128)(2,1)} %get-tuple-element.49), channel_id=1, source_target_pairs={{0,2},{2,0},{4,6},{6,4},{1,3},{3,1},{5,7},{7,5},{8,10},{10,8},{12,... | collective-permute-start | bytes 589832 | tf_op jit(solution)/shard_map/ppermute | solution.py:108
  5.3 23.5 %collective-permute-start.1 = (bf16[1,384,256]{2,1,0:T(8,128)(2,1)}, bf16[1,384,256]{2,1,0:T(8,128)(2,1)}, u32[]{:S(2)}, u32[]{:S(2)}) collective-permute-start(bf16[1,384,256]{2,1,0:T(8,128)(2,1)} %get-tuple-element.50), channel_id=1, source_target_pairs={{0,4},{2,6},{4,0},{6,2},{1,5},{3,7},{5,1},{7,3},{8,12},{10,14},{12... | collective-permute-start | bytes 589832 | tf_op jit(solution)/shard_map/ppermute | solution.py:108
  7.9 22.5 %collective-permute-start.7 = (bf16[2,384,128]{2,1,0:T(8,128)(2,1)}, bf16[2,384,128]{2,1,0:T(8,128)(2,1)}, u32[]{:S(2)}, u32[]{:S(2)}) collective-permute-start(bf16[2,384,128]{2,1,0:T(8,128)(2,1)} %get-tuple-element.57), channel_id=1, source_target_pairs={{0,2},{2,0},{4,6},{6,4},{1,3},{3,1},{5,7},{7,5},{8,10},{10,8},{12,... | collective-permute-start | bytes 589832 | tf_op jit(solution)/shard_map/ppermute | solution.py:108
  8.1 26.0 %collective-permute-start.8 = (bf16[2,384,128]{2,1,0:T(8,128)(2,1)}, bf16[2,384,128]{2,1,0:T(8,128)(2,1)}, u32[]{:S(2)}, u32[]{:S(2)}) collective-permute-start(bf16[2,384,128]{2,1,0:T(8,128)(2,1)} %get-tuple-element.58), channel_id=1, source_target_pairs={{0,4},{2,6},{4,0},{6,2},{1,5},{3,7},{5,1},{7,3},{8,12},{10,14},{12... | collective-permute-start | bytes 589832 | tf_op jit(solution)/shard_map/ppermute | solution.py:108
  8.4 9.2 %collective-permute-start.16 = (bf16[2,384,128]{2,1,0:T(8,128)(2,1)}, bf16[2,384,128]{2,1,0:T(8,128)(2,1)S(1)}, u32[]{:S(2)}, u32[]{:S(2)}) collective-permute-start(bf16[2,384,128]{2,1,0:T(8,128)(2,1)} %get-tuple-element.65), channel_id=1, source_target_pairs={{0,2},{2,0},{4,6},{6,4},{1,3},{3,1},{5,7},{7,5},{8,10},{10,8},{12,... | collective-permute-start | bytes 589832 | tf_op jit(solution)/shard_map/ppermute | solution.py:108
  14.7 12.1 %copy-start.21 = (bf16[2,384,128]{2,1,0:T(8,128)(2,1)S(1)}, bf16[2,384,128]{2,1,0:T(8,128)(2,1)}, u32[]{:S(2)}) copy-start(bf16[2,384,128]{2,1,0:T(8,128)(2,1)} %get-tuple-element.59) | copy-start | bytes 589828
  14.7 14.1 %copy-start.10 = (bf16[2,384,128]{2,1,0:T(8,128)(2,1)S(1)}, bf16[2,384,128]{2,1,0:T(8,128)(2,1)}, u32[]{:S(2)}) copy-start(bf16[2,384,128]{2,1,0:T(8,128)(2,1)} %get-tuple-element.64) | copy-start | bytes 589828
  15.8 7.8 %collective-permute-start.17 = (bf16[2,384,128]{2,1,0:T(8,128)(2,1)S(1)}, bf16[2,384,128]{2,1,0:T(8,128)(2,1)S(1)}, u32[]{:S(2)}, u32[]{:S(2)}) collective-permute-start(bf16[2,384,128]{2,1,0:T(8,128)(2,1)S(1)} %copy-done.23), channel_id=1, source_target_pairs={{0,4},{2,6},{4,0},{6,2},{1,5},{3,7},{5,1},{7,3},{8,12},{10,14},{12... | collective-permute-start | bytes 589832 | tf_op jit(solution)/shard_map/ppermute | solution.py:108
  18.2 15.8 %copy-start.20 = (bf16[1,384,256]{2,1,0:T(8,128)(2,1)S(1)}, bf16[1,384,256]{2,1,0:T(8,128)(2,1)}, u32[]{:S(2)}) copy-start(bf16[1,384,256]{2,1,0:T(8,128)(2,1)} %get-tuple-element.51) | copy-start | bytes 589828
  18.2 17.4 %copy-start.8 = (bf16[2,384,128]{2,1,0:T(8,128)(2,1)S(1)}, bf16[2,384,128]{2,1,0:T(8,128)(2,1)}, u32[]{:S(2)}) copy-start(bf16[2,384,128]{2,1,0:T(8,128)(2,1)} %get-tuple-element.56) | copy-start | bytes 589828
  18.2 8.5 %collective-permute-start.18 = (bf16[2,384,128]{2,1,0:T(8,128)(2,1)}, bf16[2,384,128]{2,1,0:T(8,128)(2,1)S(1)}, u32[]{:S(2)}, u32[]{:S(2)}) collective-permute-start(bf16[2,384,128]{2,1,0:T(8,128)(2,1)} %get-tuple-element.67), channel_id=1, source_target_pairs={{0,6},{2,4},{4,2},{6,0},{1,7},{3,5},{5,3},{7,1},{8,14},{10,12},{12... | collective-permute-start | bytes 589832 | tf_op jit(solution)/shard_map/ppermute | solution.py:108
  18.3 10.5 %copy-start.15 = (bf16[2,384,128]{2,1,0:T(8,128)(2,1)S(1)}, bf16[2,384,128]{2,1,0:T(8,128)(2,1)}, u32[]{:S(2)}) copy-start(bf16[2,384,128]{2,1,0:T(8,128)(2,1)} %copy-done.14) | copy-start | bytes 589828
  23.6 18.7 %collective-permute-start.12 = (bf16[4,128,384]{2,1,0:T(8,128)(2,1)S(1)}, bf16[4,128,384]{2,1,0:T(8,128)(2,1)S(1)}, u32[]{:S(2)}, u32[]{:S(2)}) collective-permute-start(bf16[4,128,384]{2,1,0:T(8,128)(2,1)S(1)} %get-tuple-element.93), channel_id=1, source_target_pairs={{0,1},{1,0},{2,3},{3,2},{4,5},{5,4},{6,7},{7,6},{8,9},{9,8},{10,11... | collective-permute-start | bytes 1179656 | tf_op jit(solution)/shard_map/ppermute | solution.py:355
  26.8 7.3 %collective-permute-start.9 = (bf16[2,384,128]{2,1,0:T(8,128)(2,1)S(1)}, bf16[2,384,128]{2,1,0:T(8,128)(2,1)S(1)}, u32[]{:S(2)}, u32[]{:S(2)}) collective-permute-start(bf16[2,384,128]{2,1,0:T(8,128)(2,1)S(1)} %copy-done.21), channel_id=1, source_target_pairs={{0,6},{2,4},{4,2},{6,0},{1,7},{3,5},{5,3},{7,1},{8,14},{10,12},{12... | collective-permute-start | bytes 589832 | tf_op jit(solution)/shard_map/ppermute | solution.py:108
  28.9 18.2 %copy-start.3 = (bf16[4,2,384,128]{3,2,1,0:T(8,128)(2,1)}, bf16[4,2,384,128]{3,2,1,0:T(8,128)(2,1)S(1)}, u32[]{:S(2)}) copy-start(bf16[4,2,384,128]{3,2,1,0:T(8,128)(2,1)S(1)} %pad_maximum_fusion.1.refs_9_) | copy-start | bytes 2359300
  28.9 29.7 %collective-permute-start.20 = (bf16[4,2,384,128]{3,2,1,0:T(8,128)(2,1)S(1)}, bf16[4,2,384,128]{3,2,1,0:T(8,128)(2,1)}, u32[]{:S(2)}, u32[]{:S(2)}) collective-permute-start(bf16[4,2,384,128]{3,2,1,0:T(8,128)(2,1)S(1)} %pad_maximum_fusion.1.refs_9_), channel_id=1, source_target_pairs={{8,16},{16,8},{9,17},{17,9},{10,18},{18,10},{11,19},{19,11},{12,20... | collective-permute-start | bytes 2359304 | tf_op jit(solution)/shard_map/ppermute | solution.py:118
  30.4 29.2 %collective-permute-start.19 = (bf16[4,2,384,128]{3,2,1,0:T(8,128)(2,1)S(1)}, bf16[4,2,384,128]{3,2,1,0:T(8,128)(2,1)}, u32[]{:S(2)}, u32[]{:S(2)}) collective-permute-start(bf16[4,2,384,128]{3,2,1,0:T(8,128)(2,1)S(1)} %pad_maximum_fusion.1.refs_9_), channel_id=1, source_target_pairs={{0,8},{16,24},{8,0},{24,16},{1,9},{17,25},{9,1},{25,17},{2,10},{18... | collective-permute-start | bytes 2359304 | tf_op jit(solution)/shard_map/ppermute | solution.py:118
  34.0 6.7 %collective-permute-start.2 = (bf16[1,384,256]{2,1,0:T(8,128)(2,1)S(1)}, bf16[1,384,256]{2,1,0:T(8,128)(2,1)S(1)}, u32[]{:S(2)}, u32[]{:S(2)}) collective-permute-start(bf16[1,384,256]{2,1,0:T(8,128)(2,1)S(1)} %copy-done.20), channel_id=1, source_target_pairs={{0,6},{2,4},{4,2},{6,0},{1,7},{3,5},{5,3},{7,1},{8,14},{10,12},{12... | collective-permute-start | bytes 589832 | tf_op jit(solution)/shard_map/ppermute | solution.py:108
  34.0 13.0 %collective-permute-start.3 = (bf16[4,128,384]{2,1,0:T(8,128)(2,1)S(1)}, bf16[4,128,384]{2,1,0:T(8,128)(2,1)}, u32[]{:S(2)}, u32[]{:S(2)}) collective-permute-start(bf16[4,128,384]{2,1,0:T(8,128)(2,1)S(1)} %get-tuple-element.94), channel_id=1, source_target_pairs={{0,1},{1,0},{2,3},{3,2},{4,5},{5,4},{6,7},{7,6},{8,9},{9,8},{10,11... | collective-permute-start | bytes 1179656 | tf_op jit(solution)/shard_map/ppermute | solution.py:355
  36.7 19.9 %copy-start.2 = (bf16[4,2,384,128]{3,2,1,0:T(8,128)(2,1)}, bf16[4,2,384,128]{3,2,1,0:T(8,128)(2,1)S(1)}, u32[]{:S(2)}) copy-start(bf16[4,2,384,128]{3,2,1,0:T(8,128)(2,1)S(1)} %pad_maximum_fusion.refs_9_) | copy-start | bytes 2359300
  40.7 35.4 %collective-permute-start.11 = (bf16[4,2,384,128]{3,2,1,0:T(8,128)(2,1)S(1)}, bf16[4,2,384,128]{3,2,1,0:T(8,128)(2,1)}, u32[]{:S(2)}, u32[]{:S(2)}) collective-permute-start(bf16[4,2,384,128]{3,2,1,0:T(8,128)(2,1)S(1)} %pad_maximum_fusion.refs_9_), channel_id=1, source_target_pairs={{8,16},{16,8},{9,17},{17,9},{10,18},{18,10},{11,19},{19,11},{12,20... | collective-permute-start | bytes 2359304 | tf_op jit(solution)/shard_map/ppermute | solution.py:118
  42.3 33.9 %collective-permute-start.10 = (bf16[4,2,384,128]{3,2,1,0:T(8,128)(2,1)S(1)}, bf16[4,2,384,128]{3,2,1,0:T(8,128)(2,1)}, u32[]{:S(2)}, u32[]{:S(2)}) collective-permute-start(bf16[4,2,384,128]{3,2,1,0:T(8,128)(2,1)S(1)} %pad_maximum_fusion.refs_9_), channel_id=1, source_target_pairs={{0,8},{16,24},{8,0},{24,16},{1,9},{17,25},{9,1},{25,17},{2,10},{18... | collective-permute-start | bytes 2359304 | tf_op jit(solution)/shard_map/ppermute | solution.py:118
  47.1 1.6 %collective-permute-start.13 = (bf16[128,384]{1,0:T(8,128)(2,1)}, bf16[128,384]{1,0:T(8,128)(2,1)S(1)}, u32[]{:S(2)}, u32[]{:S(2)}) collective-permute-start(bf16[128,384]{1,0:T(8,128)(2,1)} %get-tuple-element.61), channel_id=1, source_target_pairs={{0,2},{2,0},{4,6},{6,4},{1,3},{3,1},{5,7},{7,5},{8,10},{10,8},{12,... | collective-permute-start | bytes 294920 | tf_op jit(solution)/shard_map/ppermute | solution.py:108
  48.6 11.8 %copy-start.27 = (bf16[128,384]{1,0:T(8,128)(2,1)}, bf16[128,384]{1,0:T(8,128)(2,1)S(1)}, u32[]{:S(2)}) copy-start(bf16[128,384]{1,0:T(8,128)(2,1)S(1)} %collective-permute-done.13.refs_5_) | copy-start | bytes 294916
  48.6 5.1 %collective-permute-start.14 = (bf16[128,384]{1,0:T(8,128)(2,1)}, bf16[128,384]{1,0:T(8,128)(2,1)S(1)}, u32[]{:S(2)}, u32[]{:S(2)}) collective-permute-start(bf16[128,384]{1,0:T(8,128)(2,1)} %get-tuple-element.62), channel_id=1, source_target_pairs={{0,4},{2,6},{4,0},{6,2},{1,5},{3,7},{5,1},{7,3},{8,12},{10,14},{12... | collective-permute-start | bytes 294920 | tf_op jit(solution)/shard_map/ppermute | solution.py:108
  53.7 4.9 %collective-permute-start.15 = (bf16[128,384]{1,0:T(8,128)(2,1)}, bf16[128,384]{1,0:T(8,128)(2,1)S(1)}, u32[]{:S(2)}, u32[]{:S(2)}) collective-permute-start(bf16[128,384]{1,0:T(8,128)(2,1)} %get-tuple-element.63), channel_id=1, source_target_pairs={{0,6},{2,4},{4,2},{6,0},{1,7},{3,5},{5,3},{7,1},{8,14},{10,12},{12... | collective-permute-start | bytes 294920 | tf_op jit(solution)/shard_map/ppermute | solution.py:108
  58.6 14.3 %collective-permute-start.4 = (bf16[128,384]{1,0:T(8,128)(2,1)}, bf16[128,384]{1,0:T(8,128)(2,1)S(1)}, u32[]{:S(2)}, u32[]{:S(2)}) collective-permute-start(bf16[128,384]{1,0:T(8,128)(2,1)} %get-tuple-element.53), channel_id=1, source_target_pairs={{0,2},{2,0},{4,6},{6,4},{1,3},{3,1},{5,7},{7,5},{8,10},{10,8},{12,... | collective-permute-start | bytes 294920 | tf_op jit(solution)/shard_map/ppermute | solution.py:108
  58.6 16.8 %collective-permute-start.5 = (bf16[128,384]{1,0:T(8,128)(2,1)}, bf16[128,384]{1,0:T(8,128)(2,1)S(1)}, u32[]{:S(2)}, u32[]{:S(2)}) collective-permute-start(bf16[128,384]{1,0:T(8,128)(2,1)} %get-tuple-element.54), channel_id=1, source_target_pairs={{0,4},{2,6},{4,0},{6,2},{1,5},{3,7},{5,1},{7,3},{8,12},{10,14},{12... | collective-permute-start | bytes 294920 | tf_op jit(solution)/shard_map/ppermute | solution.py:108
  59.7 16.5 %collective-permute-start.6 = (bf16[128,384]{1,0:T(8,128)(2,1)}, bf16[128,384]{1,0:T(8,128)(2,1)S(1)}, u32[]{:S(2)}, u32[]{:S(2)}) collective-permute-start(bf16[128,384]{1,0:T(8,128)(2,1)} %get-tuple-element.55), channel_id=1, source_target_pairs={{0,6},{2,4},{4,2},{6,0},{1,7},{3,5},{5,3},{7,1},{8,14},{10,12},{12... | collective-permute-start | bytes 294920 | tf_op jit(solution)/shard_map/ppermute | solution.py:108
  72.9 23.4 %collective-permute-start.24 = (bf16[4,2,384,128]{3,2,1,0:T(8,128)(2,1)}, bf16[4,2,384,128]{3,2,1,0:T(8,128)(2,1)S(1)}, u32[]{:S(2)}, u32[]{:S(2)}) collective-permute-start(bf16[4,2,384,128]{3,2,1,0:T(8,128)(2,1)} %get-tuple-element.77), channel_id=1, source_target_pairs={{0,8},{16,24},{8,0},{24,16},{1,9},{17,25},{9,1},{25,17},{2,10},{18... | collective-permute-start | bytes 2359304 | tf_op jit(solution)/shard_map/ppermute | solution.py:118
  75.4 22.2 %collective-permute-start.25 = (bf16[4,2,384,128]{3,2,1,0:T(8,128)(2,1)}, bf16[4,2,384,128]{3,2,1,0:T(8,128)(2,1)S(1)}, u32[]{:S(2)}, u32[]{:S(2)}) collective-permute-start(bf16[4,2,384,128]{3,2,1,0:T(8,128)(2,1)} %get-tuple-element.78), channel_id=1, source_target_pairs={{8,16},{16,8},{9,17},{17,9},{10,18},{18,10},{11,19},{19,11},{12,20... | collective-permute-start | bytes 2359304 | tf_op jit(solution)/shard_map/ppermute | solution.py:118
  89.5 23.2 %collective-permute-start.29 = (bf16[4,2,384,128]{3,2,1,0:T(8,128)(2,1)}, bf16[4,2,384,128]{3,2,1,0:T(8,128)(2,1)S(1)}, u32[]{:S(2)}, u32[]{:S(2)}) collective-permute-start(bf16[4,2,384,128]{3,2,1,0:T(8,128)(2,1)} %get-tuple-element.84), channel_id=1, source_target_pairs={{0,8},{16,24},{8,0},{24,16},{1,9},{17,25},{9,1},{25,17},{2,10},{18... | collective-permute-start | bytes 2359304 | tf_op jit(solution)/shard_map/ppermute | solution.py:118
  94.7 18.0 %collective-permute-start.30 = (bf16[4,2,384,128]{3,2,1,0:T(8,128)(2,1)}, bf16[4,2,384,128]{3,2,1,0:T(8,128)(2,1)}, u32[]{:S(2)}, u32[]{:S(2)}) collective-permute-start(bf16[4,2,384,128]{3,2,1,0:T(8,128)(2,1)} %get-tuple-element.85), channel_id=1, source_target_pairs={{8,16},{16,8},{9,17},{17,9},{10,18},{18,10},{11,19},{19,11},{12,20... | collective-permute-start | bytes 2359304 | tf_op jit(solution)/shard_map/ppermute | solution.py:118
  96.3 20.3 %collective-permute-start.21 = (bf16[2,384,128]{2,1,0:T(8,128)(2,1)}, bf16[2,384,128]{2,1,0:T(8,128)(2,1)}, u32[]{:S(2)}, u32[]{:S(2)}) collective-permute-start(bf16[2,384,128]{2,1,0:T(8,128)(2,1)} %get-tuple-element.73), channel_id=1, source_target_pairs={{0,2},{2,0},{4,6},{6,4},{1,3},{3,1},{5,7},{7,5},{8,10},{10,8},{12,... | collective-permute-start | bytes 589832 | tf_op jit(solution)/shard_map/ppermute | solution.py:108
  96.3 21.0 %collective-permute-start.22 = (bf16[2,384,128]{2,1,0:T(8,128)(2,1)}, bf16[2,384,128]{2,1,0:T(8,128)(2,1)}, u32[]{:S(2)}, u32[]{:S(2)}) collective-permute-start(bf16[2,384,128]{2,1,0:T(8,128)(2,1)} %get-tuple-element.74), channel_id=1, source_target_pairs={{0,4},{2,6},{4,0},{6,2},{1,5},{3,7},{5,1},{7,3},{8,12},{10,14},{12... | collective-permute-start | bytes 589832 | tf_op jit(solution)/shard_map/ppermute | solution.py:108
  97.6 20.0 %collective-permute-start.23 = (bf16[2,384,128]{2,1,0:T(8,128)(2,1)}, bf16[2,384,128]{2,1,0:T(8,128)(2,1)}, u32[]{:S(2)}, u32[]{:S(2)}) collective-permute-start(bf16[2,384,128]{2,1,0:T(8,128)(2,1)} %get-tuple-element.75), channel_id=1, source_target_pairs={{0,6},{2,4},{4,2},{6,0},{1,7},{3,5},{5,3},{7,1},{8,14},{10,12},{12... | collective-permute-start | bytes 589832 | tf_op jit(solution)/shard_map/ppermute | solution.py:108
  101.1 15.6 %copy-start.22 = (bf16[2,384,128]{2,1,0:T(8,128)(2,1)S(1)}, bf16[2,384,128]{2,1,0:T(8,128)(2,1)}, u32[]{:S(2)}) copy-start(bf16[2,384,128]{2,1,0:T(8,128)(2,1)} %get-tuple-element.82) | copy-start | bytes 589828
  112.8 6.1 %collective-permute-start.26 = (bf16[2,384,128]{2,1,0:T(8,128)(2,1)}, bf16[2,384,128]{2,1,0:T(8,128)(2,1)S(1)}, u32[]{:S(2)}, u32[]{:S(2)}) collective-permute-start(bf16[2,384,128]{2,1,0:T(8,128)(2,1)} %get-tuple-element.80), channel_id=1, source_target_pairs={{0,2},{2,0},{4,6},{6,4},{1,3},{3,1},{5,7},{7,5},{8,10},{10,8},{12,... | collective-permute-start | bytes 589832 | tf_op jit(solution)/shard_map/ppermute | solution.py:108
  112.8 8.0 %collective-permute-start.27 = (bf16[2,384,128]{2,1,0:T(8,128)(2,1)}, bf16[2,384,128]{2,1,0:T(8,128)(2,1)S(1)}, u32[]{:S(2)}, u32[]{:S(2)}) collective-permute-start(bf16[2,384,128]{2,1,0:T(8,128)(2,1)} %get-tuple-element.81), channel_id=1, source_target_pairs={{0,4},{2,6},{4,0},{6,2},{1,5},{3,7},{5,1},{7,3},{8,12},{10,14},{12... | collective-permute-start | bytes 589832 | tf_op jit(solution)/shard_map/ppermute | solution.py:108
  116.6 7.3 %collective-permute-start.28 = (bf16[2,384,128]{2,1,0:T(8,128)(2,1)S(1)}, bf16[2,384,128]{2,1,0:T(8,128)(2,1)S(1)}, u32[]{:S(2)}, u32[]{:S(2)}) collective-permute-start(bf16[2,384,128]{2,1,0:T(8,128)(2,1)S(1)} %copy-done.22), channel_id=1, source_target_pairs={{0,6},{2,4},{4,2},{6,0},{1,7},{3,5},{5,3},{7,1},{8,14},{10,12},{12... | collective-permute-start | bytes 589832 | tf_op jit(solution)/shard_map/ppermute | solution.py:108
  117.3 6.7 %collective-permute-start.31 = (bf16[2,384,128]{2,1,0:T(8,128)(2,1)}, bf16[2,384,128]{2,1,0:T(8,128)(2,1)S(1)}, u32[]{:S(2)}, u32[]{:S(2)}) collective-permute-start(bf16[2,384,128]{2,1,0:T(8,128)(2,1)} %get-tuple-element.87), channel_id=1, source_target_pairs={{0,2},{2,0},{4,6},{6,4},{1,3},{3,1},{5,7},{7,5},{8,10},{10,8},{12,... | collective-permute-start | bytes 589832 | tf_op jit(solution)/shard_map/ppermute | solution.py:108
  117.6 11.6 %collective-permute-start.32 = (bf16[2,384,128]{2,1,0:T(8,128)(2,1)}, bf16[2,384,128]{2,1,0:T(8,128)(2,1)S(1)}, u32[]{:S(2)}, u32[]{:S(2)}) collective-permute-start(bf16[2,384,128]{2,1,0:T(8,128)(2,1)} %get-tuple-element.88), channel_id=1, source_target_pairs={{0,4},{2,6},{4,0},{6,2},{1,5},{3,7},{5,1},{7,3},{8,12},{10,14},{12... | collective-permute-start | bytes 589832 | tf_op jit(solution)/shard_map/ppermute | solution.py:108
  118.8 13.6 %copy-start.9 = (bf16[2,384,128]{2,1,0:T(8,128)(2,1)}, bf16[2,384,128]{2,1,0:T(8,128)(2,1)S(1)}, u32[]{:S(2)}) copy-start(bf16[2,384,128]{2,1,0:T(8,128)(2,1)S(1)} %collective-permute-done.26.refs_5_) | copy-start | bytes 589828
  118.8 13.6 %collective-permute-start.33 = (bf16[2,384,128]{2,1,0:T(8,128)(2,1)}, bf16[2,384,128]{2,1,0:T(8,128)(2,1)S(1)}, u32[]{:S(2)}, u32[]{:S(2)}) collective-permute-start(bf16[2,384,128]{2,1,0:T(8,128)(2,1)} %get-tuple-element.89), channel_id=1, source_target_pairs={{0,6},{2,4},{4,2},{6,0},{1,7},{3,5},{5,3},{7,1},{8,14},{10,12},{12... | collective-permute-start | bytes 589832 | tf_op jit(solution)/shard_map/ppermute | solution.py:108
  120.8 11.6 %copy-start.11 = (bf16[2,384,128]{2,1,0:T(8,128)(2,1)}, bf16[2,384,128]{2,1,0:T(8,128)(2,1)S(1)}, u32[]{:S(2)}) copy-start(bf16[2,384,128]{2,1,0:T(8,128)(2,1)S(1)} %collective-permute-done.27.refs_6_) | copy-start | bytes 589828
  124.0 8.4 %copy-start.12 = (bf16[2,384,128]{2,1,0:T(8,128)(2,1)}, bf16[2,384,128]{2,1,0:T(8,128)(2,1)S(1)}, u32[]{:S(2)}) copy-start(bf16[2,384,128]{2,1,0:T(8,128)(2,1)S(1)} %collective-permute-done.28.refs_7_) | copy-start | bytes 589828
  124.0 8.4 %copy-start.13 = (bf16[2,384,128]{2,1,0:T(8,128)(2,1)}, bf16[2,384,128]{2,1,0:T(8,128)(2,1)S(1)}, u32[]{:S(2)}) copy-start(bf16[2,384,128]{2,1,0:T(8,128)(2,1)S(1)} %collective-permute-done.31.refs_9_) | copy-start | bytes 589828
  (16 other events, 32.9 us)
